TPU v7x, 32 devices: a whole 2x2x4 slice. The times are simulated.
32 devices in a mesh: groups: 2 (over y), wide: 4 (over z), heads: 4 (over x, core).
Axes of the slice: x: 2, y: 2, z: 4, core: 2. Of those that a mesh axis runs over, the one named last changes fastest.
Arguments:
- video_hidden: bfloat16 [2048, 4096], P(('groups', 'wide'), 'heads'), parts along dimension 0, may hold values from -6 to 6
- audio_hidden: bfloat16 [512, 2048], P(('groups', 'wide'), 'heads'), parts along dimension 0, may hold values from -6 to 6
- video_query: bfloat16 [2048, 2048], P(('groups', 'wide'), 'heads'), parts along dimension 0, may hold values from -8 to 8
- video_key: bfloat16 [2048, 2048], P(('groups', 'wide'), 'heads'), parts along dimension 0, may hold values from -8 to 8
- video_value: bfloat16 [2048, 2048], P(('groups', 'wide'), 'heads'), parts along dimension 0, may hold values from -6 to 6
- audio_query: bfloat16 [512, 1024], P(('groups', 'wide'), 'heads'), parts along dimension 0, may hold values from -8 to 8
- audio_key: bfloat16 [512, 1024], P(('groups', 'wide'), 'heads'), parts along dimension 0, may hold values from -8 to 8
- audio_value: bfloat16 [512, 1024], P(('groups', 'wide'), 'heads'), parts along dimension 0, may hold values from -6 to 6
- cross_video_query: bfloat16 [2048, 1024], P(('groups', 'wide'), 'heads'), parts along dimension 0, may hold values from -8 to 8
- cross_audio_key: bfloat16 [512, 1024], P(('groups', 'wide'), 'heads'), parts along dimension 0, may hold values from -8 to 8
- cross_audio_value: bfloat16 [512, 1024], P(('groups', 'wide'), 'heads'), parts along dimension 0, may hold values from -6 to 6
- cross_audio_query: bfloat16 [512, 1024], P(('groups', 'wide'), 'heads'), parts along dimension 0, may hold values from -8 to 8
- cross_video_key: bfloat16 [2048, 1024], P(('groups', 'wide'), 'heads'), parts along dimension 0, may hold values from -8 to 8
- cross_video_value: bfloat16 [2048, 1024], P(('groups', 'wide'), 'heads'), parts along dimension 0, may hold values from -6 to 6
- video_self_out: bfloat16 [2048, 4096], P('heads', 'wide'), may hold values from -0.125 to 0.125
- video_cross_out: bfloat16 [1024, 4096], P('heads', 'wide'), may hold values from -0.1875 to 0.1875
- audio_self_out: bfloat16 [1024, 2048], P('heads', 'wide'), may hold values from -0.1875 to 0.1875
- audio_cross_out: bfloat16 [1024, 2048], P('heads', 'wide'), may hold values from -0.1875 to 0.1875
- intersection: int32 [8, 5], P('groups'), parts along dimension 0, may hold values from 0 to 1, as said below
Outputs:
- video_out: bfloat16 [2048, 4096], P(('groups', 'wide'), 'heads'), parts along dimension 0
- audio_out: bfloat16 [512, 2048], P(('groups', 'wide'), 'heads'), parts along dimension 0
There are 2 independent parts, one for each index of `groups`. A program takes and returns all parts, laid end to end along the dimension named above; an argument that names none is the same for every part. Nothing has to cross between parts.
Inputs may be any that keep to these rules, and one draw needn't show every extreme that they name: `intersection`: column 2 is 1 in every row; entries that would pair a block with one outside the clip are ignored.
All inputs are finite; a program needn't handle non-finite values.
Results may differ from a plain program's by a relative error of at most 0.012.
Values may be sent and summed in bfloat16 or wider, within the bound.
A program may use at most 64 MiB of HBM per device.

v0:
```python
import functools
import math

import jax
import jax.numpy as jnp
from jax import lax
from jax.experimental import pallas as pl
from jax.experimental.pallas import tpu as pltpu
from jax.sharding import PartitionSpec as P

HDV = 128
HDA = 64
REACH = 2


def passed_along(value, axis, by):
    length = lax.axis_size(axis)
    pairs = [(i, i + by) for i in range(length) if 0 <= i + by < length]
    return lax.ppermute(value, axis, pairs)


def empty_state(row_count, head_count, head_size):
    return (
        jnp.full((head_count, row_count), -1e30, jnp.float32),
        jnp.zeros((head_count, row_count), jnp.float32),
        jnp.zeros((head_count, row_count, head_size), jnp.float32),
    )


def absorb(state, queries, key_rows, value_rows, head_size, allowed):
    maxima, totals, running = state
    head_count = queries.shape[1] // head_size
    query_heads = queries.reshape(queries.shape[0], head_count, head_size)
    key_heads = key_rows.reshape(key_rows.shape[0], head_count, head_size)
    value_heads = value_rows.reshape(value_rows.shape[0], head_count, head_size)
    scores = jnp.einsum(
        "qhd,khd->hqk", query_heads, key_heads, preferred_element_type=jnp.float32
    ) * (1.0 / math.sqrt(head_size))
    if allowed is not None:
        scores = jnp.where(allowed[None, None, :], scores, -1e30)
    new_peak = jnp.maximum(maxima, jnp.max(scores, axis=2))
    weights = jnp.exp(scores - new_peak[:, :, None])
    if allowed is not None:
        weights = jnp.where(allowed[None, None, :], weights, 0.0)
    rescale = jnp.exp(maxima - new_peak)
    totals = totals * rescale + jnp.sum(weights, axis=2)
    running = running * rescale[:, :, None] + jnp.einsum(
        "hqk,khd->hqd",
        weights.astype(jnp.bfloat16),
        value_heads,
        preferred_element_type=jnp.float32,
    )
    return (new_peak, totals, running)


def finish(state, head_size):
    maxima, totals, running = state
    result = running / totals[:, :, None]
    return (
        result.transpose(1, 0, 2)
        .reshape(result.shape[1], result.shape[0] * head_size)
        .astype(jnp.bfloat16)
    )


def permitted(key_blocks, position, table_row, wide_count):
    offsets = key_blocks - position + REACH
    matches = (offsets[:, None] == jnp.arange(2 * REACH + 1, dtype=jnp.int32)[None, :]) & (
        table_row[None, :] > 0
    )
    inside = (key_blocks >= 0) & (key_blocks < wide_count)
    return jnp.any(matches, axis=1) & inside


def general_shards(
    video_hidden,
    audio_hidden,
    video_query,
    video_key,
    video_value,
    audio_query,
    audio_key,
    audio_value,
    cross_video_query,
    cross_audio_key,
    cross_audio_value,
    cross_audio_query,
    cross_video_key,
    cross_video_value,
    video_self_out,
    video_cross_out,
    audio_self_out,
    audio_cross_out,
    intersection,
):
    position = lax.axis_index("wide")
    wide_count = lax.axis_size("wide")
    video_count = video_query.shape[0]
    audio_count = audio_query.shape[0]
    head_count = video_query.shape[1] // HDV
    video_start = empty_state(video_count, head_count, HDV)
    audio_start = empty_state(audio_count, head_count, HDA)
    carried = (video_start, audio_start)
    portion = (
        lax.all_gather(video_key, "wide", axis=0, tiled=True),
        lax.all_gather(video_value, "wide", axis=0, tiled=True),
        lax.all_gather(audio_key, "wide", axis=0, tiled=True),
        lax.all_gather(audio_value, "wide", axis=0, tiled=True),
    )
    video_state = absorb(carried[0], video_query, portion[0], portion[1], HDV, None)
    audio_state = absorb(carried[1], audio_query, portion[2], portion[3], HDA, None)
    table_row = lax.dynamic_slice_in_dim(intersection, position, 1, 0)[0]
    padded_table = jnp.pad(intersection, ((REACH, REACH), (0, 0)))
    flag_row = jnp.diagonal(
        jnp.fliplr(lax.dynamic_slice_in_dim(padded_table, position, 2 * REACH + 1, 0))
    )
    stacked = jnp.concatenate(
        [cross_audio_key, cross_audio_value, cross_video_key, cross_video_value], 0
    )

    def take_cross(carried, portion, block):
        audio_keys = portion[:audio_count]
        audio_values = portion[audio_count : 2 * audio_count]
        video_keys = portion[2 * audio_count : 2 * audio_count + video_count]
        video_values = portion[2 * audio_count + video_count :]
        audio_blocks = jnp.full((audio_count,), block, jnp.int32)
        video_blocks = jnp.full((video_count,), block, jnp.int32)
        return (
            absorb(
                carried[0],
                cross_video_query,
                audio_keys,
                audio_values,
                HDA,
                permitted(audio_blocks, position, table_row, wide_count),
            ),
            absorb(
                carried[1],
                cross_audio_query,
                video_keys,
                video_values,
                HDA,
                permitted(video_blocks, position, flag_row, wide_count),
            ),
        )

    cross_start = (
        empty_state(video_count, head_count, HDA),
        empty_state(audio_count, head_count, HDA),
    )
    carried = take_cross(cross_start, stacked, position)
    for offset in range(-REACH, REACH + 1):
        if offset != 0:
            nearby = passed_along(stacked, "wide", -offset)
            carried = take_cross(carried, nearby, position + offset)
    to_video, to_audio = carried
    video_joined = jnp.concatenate([finish(video_state, HDV), finish(to_video, HDA)], 1)
    audio_joined = jnp.concatenate([finish(audio_state, HDA), finish(to_audio, HDA)], 1)
    video_weights = jnp.concatenate([video_self_out, video_cross_out], 0)
    audio_weights = jnp.concatenate([audio_self_out, audio_cross_out], 0)
    video_terms = jnp.dot(
        video_joined,
        lax.all_gather(video_weights, "wide", axis=1, tiled=True),
        preferred_element_type=jnp.float32,
    )
    audio_terms = jnp.dot(
        audio_joined,
        lax.all_gather(audio_weights, "wide", axis=1, tiled=True),
        preferred_element_type=jnp.float32,
    )
    video_sum, audio_sum = (
        lax.psum_scatter(
            video_terms.astype(jnp.bfloat16), "heads", scatter_dimension=1, tiled=True
        ).astype(jnp.float32),
        lax.psum_scatter(
            audio_terms.astype(jnp.bfloat16), "heads", scatter_dimension=1, tiled=True
        ).astype(jnp.float32),
    )
    video_out = (video_hidden.astype(jnp.float32) + video_sum).astype(jnp.bfloat16)
    audio_out = (audio_hidden.astype(jnp.float32) + audio_sum).astype(jnp.bfloat16)
    return (video_out, audio_out)


NT = (((1,), (1,)), ((), ()))
MESH = pl.DeviceIdType.MESH


def pack_kernel(
    n, cvq, cvk, cvv, aq, ak, av, caq, cak, cav, aso, aco, table, pack, wa, bias_v, bias_a
):
    rows = cvq.shape[0]
    half = rows // 2
    few = aq.shape[0]
    for i in range(n):
        for j in range(n):
            column = j - i + REACH
            drop = jnp.float32(-1e30)
            if 0 <= column < table.shape[1]:
                drop = jnp.where(table[i, column] > 0, jnp.float32(0.0), drop)
            bias_v[i : i + 1, j * few : (j + 1) * few] = jnp.full((1, few), drop)
            bias_a[j : j + 1, i * rows : (i + 1) * rows] = jnp.full((1, rows), drop)
    for j in range(n):
        cols = slice(j * HDA, (j + 1) * HDA)
        pack[j, :rows, :] = jnp.concatenate([cvq[:, cols], cvk[:, cols]], 1)
        pack[j, rows : rows + half, :] = jnp.concatenate([cvv[:half, cols], cvv[half:, cols]], 1)
        at = rows + half
        for left, right in ((aq, ak), (av, caq), (cak, cav)):
            pack[j, at : at + few, :] = jnp.concatenate([left[:, cols], right[:, cols]], 1)
            at += few
        wa[2 * j * HDA : (2 * j + 1) * HDA, :] = aso[cols, :]
        wa[(2 * j + 1) * HDA : (2 * j + 2) * HDA, :] = aco[cols, :]


def attend(queries, keys, values, head_size, bias):
    scores = lax.dot_general(queries, keys, NT, preferred_element_type=jnp.float32)
    scores = scores * (1.0 / math.sqrt(head_size))
    if bias is not None:
        scores = scores + bias
    weights = jnp.exp(scores - jnp.max(scores, axis=1, keepdims=True))
    totals = jnp.sum(weights, axis=1, keepdims=True)
    mixed = jnp.dot(weights.astype(jnp.bfloat16), values, preferred_element_type=jnp.float32)
    return (mixed / totals).astype(jnp.bfloat16)


def fused_kernel(
    n, chunks,
    vq, vk, vv, pack, ws, wc, wa, bias_v, bias_a,
    out_v, out_a,
    q_all, k_all, v_all, p_all, ws_all, wc_all, wa_all,
    o_self, o_rest, r_self, r_rest, sum_v, sum_a, mid_v, mid_a,
    a_send, a_recv, w_send, w_recv, f_send, f_recv, x_send, x_recv, z_send, z_recv,
    d_send, d_recv, e_send, e_recv, local,
):
    w = lax.axis_index("wide")
    h = lax.axis_index("heads")
    rows = vq.shape[0]
    half = rows // 2
    few = out_a.shape[0]
    part_rows, part_few = rows // n, few // n

    def place(dw, dh):
        return {"wide": lax.rem(w + dw, n), "heads": lax.rem(h + dh, n)}

    def remote(source, target, send, recv, device):
        return pltpu.make_async_remote_copy(
            src_ref=source, dst_ref=target, send_sem=send, recv_sem=recv,
            device_id=device, device_id_type=MESH,
        )

    others = [(d, 0) for d in range(1, n)] + [(0, d) for d in range(1, n)]
    barrier = pltpu.get_barrier_semaphore()
    for dw, dh in others:
        pl.semaphore_signal(barrier, inc=1, device_id=place(dw, dh), device_id_type=MESH)

    def head_cols(ref, who):
        return ref.at[:, pl.ds(pl.multiple_of(who * HDV, HDV), HDV)]

    own = [pltpu.make_async_copy(pack.at[w], p_all.at[w], local.at[0])]
    for i, (source, target) in enumerate(((vk, k_all), (vv, v_all), (vq, q_all))):
        own.append(pltpu.make_async_copy(head_cols(source, w), target.at[w], local.at[1 + i]))
    for i, (source, target) in enumerate(((ws, ws_all), (wc, wc_all), (wa, wa_all))):
        own.append(pltpu.make_async_copy(source, target.at[h], local.at[4 + i]))
    for copy in own:
        copy.start()
    pl.semaphore_wait(barrier, len(others))

    a_copies = {}
    for i, (source, target) in enumerate(((pack, p_all), (vk, k_all), (vv, v_all), (vq, q_all))):
        for d in range(1, n):
            who = lax.rem(w + d, n)
            piece = source.at[who] if i == 0 else head_cols(source, who)
            copy = remote(piece, target.at[w], a_send.at[i, d], a_recv.at[i, d], place(d, 0))
            copy.start()
            a_copies[i, d] = copy

    pairs = ((ws, ws_all), (wc, wc_all), (wa, wa_all))
    partner = {"wide": w, "heads": h + 1 - 2 * lax.rem(h, 2)}
    w_copies, f_copies = [[], [], []], [[], [], []]

    def send_weights(i):
        source, target = pairs[i]
        for k in range(1, n // 2):
            copy = remote(source, target.at[h], w_send.at[i, k], w_recv.at[i, k], place(0, 2 * k))
            copy.start()
            w_copies[i].append(copy)

    def pass_weights(i):
        target = pairs[i][1]
        for k in range(1, n // 2):
            w_copies[i][k - 1].wait_recv()
            slot = lax.rem(h + n - 2 * k, n)
            copy = remote(target.at[slot], target.at[slot], f_send.at[i, k], f_recv.at[i, k], partner)
            copy.start()
            f_copies[i].append(copy)

    def settle_weights(i):
        own[4 + i].wait()
        for copy in f_copies[i]:
            copy.wait_recv()

    send_weights(0)
    for i, (source, target) in enumerate(pairs):
        copy = remote(source, target.at[h], f_send.at[i, 0], f_recv.at[i, 0], partner)
        copy.start()
        f_copies[i].append(copy)

    own[0].wait()
    for d in range(1, n):
        a_copies[0, d].wait_recv()
    at = rows + half

    def part(j, start, right):
        return p_all[j, start : start + few, HDA:] if right else p_all[j, start : start + few, :HDA]

    def whole(start, right):
        return jnp.concatenate([part(j, start, right) for j in range(n)], 0)

    aq, ak = whole(at, False), whole(at, True)
    av, caq = whole(at + few, False), whole(at + few, True)
    cak, cav = whole(at + 2 * few, False), whole(at + 2 * few, True)
    cvk = jnp.concatenate([p_all[j, :rows, HDA:] for j in range(n)], 0)
    cvv = jnp.concatenate(
        [p_all[j, rows:at, cols] for j in range(n) for cols in (slice(0, HDA), slice(HDA, 2 * HDA))], 0
    )
    wide_bias = jnp.concatenate(
        [jnp.broadcast_to(bias_a[j : j + 1, :], (few, bias_a.shape[1])) for j in range(n)], 0
    )
    audio = jnp.concatenate(
        [attend(aq, ak, av, HDA, None), attend(caq, cvk, cvv, HDA, wide_bias)], 1
    )
    tall_bias = jnp.concatenate(
        [jnp.broadcast_to(bias_v[j : j + 1, :], (part_rows, bias_v.shape[1])) for j in range(n)], 0
    )
    for t in range(n):
        queries = jnp.concatenate(
            [p_all[j, t * part_rows : (t + 1) * part_rows, :HDA] for j in range(n)], 0
        )
        o_rest[t, half:, :] = jnp.concatenate(
            [audio[j * few + t * part_few : j * few + (t + 1) * part_few, :] for j in range(n)], 0
        )
        mixed = attend(queries, cak, cav, HDA, tall_bias)
        o_rest[t, :half, :] = jnp.concatenate([mixed[:half], mixed[half:]], 1)

    mine = h * n + w
    buffers = ((o_rest, r_rest), (o_self, r_self))
    x_copies = {}
    steps = n - 1

    def across(kind, d):
        source, landing = buffers[kind]
        copy = remote(
            source.at[lax.rem(h + d, n)], landing.at[mine],
            x_send.at[kind, d], x_recv.at[kind, d], place(0, d),
        )
        copy.start()
        x_copies[kind, d] = copy

    def along(kind, d, step, way):
        source, landing = buffers[kind]
        slot = lax.rem(h + n - d, n) * n + w - way * step
        piece = source.at[h] if d == 0 and step == 0 else landing.at[slot]
        at = (((way + 1) // 2 * steps + step) * 2 + kind) * n + d
        return remote(
            piece, landing.at[slot], z_send.at[at], z_recv.at[at],
            {"wide": w + way, "heads": h},
        )

    def sends(step, way):
        if way > 0:
            return (w >= step) & (w < n - 1)
        return (w + step < n) & (w > 0)

    def forward(kind, d, step):
        for way in (1, -1):
            if step:
                gather(kind, d, step - 1, way)

            @pl.when(sends(step, way))
            def _():
                along(kind, d, step, way).start()

    def gather(kind, d, step, way):
        arrives = (w >= step + 1) if way > 0 else (w + step + 1 < n)

        @pl.when(arrives)
        def _():
            landing = buffers[kind][1]
            at = (((way + 1) // 2 * steps + step) * 2 + kind) * n + d
            slot = lax.rem(h + n - d, n) * n + w - way * (step + 1)
            remote(
                landing.at[slot], landing.at[slot], z_send.at[at], z_recv.at[at],
                {"wide": w - way, "heads": h},
            ).wait_recv()

    for d in range(1, n):
        across(0, d)
    send_weights(1)
    forward(0, 0, 0)
    r_rest[pl.ds(mine, 1)] = o_rest[pl.ds(h, 1)]
    for d in range(1, n):
        x_copies[0, d].wait_recv()
        forward(0, d, 0)

    for i in range(1, 4):
        own[i].wait()
        for d in range(1, n):
            a_copies[i, d].wait_recv()
    keys = k_all[...].reshape(n * rows, HDV)
    values = v_all[...].reshape(n * rows, HDV)
    for d in range(n):
        block = lax.rem(h + d, n)
        start = pl.multiple_of(block * part_rows, part_rows)
        queries = q_all[:, pl.ds(start, part_rows), :].reshape(rows, HDV)
        o_self[pl.ds(block, 1)] = attend(queries, keys, values, HDV, None)[None]
        if d:
            across(1, d)
        else:
            forward(1, 0, 0)
            r_self[pl.ds(mine, 1)] = o_self[pl.ds(h, 1)]
        if d > 1:
            x_copies[1, d - 1].wait_recv()
            forward(1, d - 1, 0)
        if steps > 1:
            forward(0, d, 1)
    x_copies[1, n - 1].wait_recv()
    forward(1, n - 1, 0)

    send_weights(2)
    pass_weights(0)
    pass_weights(1)

    for kind in range(2):
        for step in range(2 - kind, steps):
            for d in range(n):
                forward(kind, d, step)
    for kind in range(2):
        for d in range(n):
            for way in (1, -1):
                gather(kind, d, steps - 1, way)

    pass_weights(2)
    settle_weights(0)
    settle_weights(1)

    heads = n * n
    joined = jnp.concatenate([r_self[s] for s in range(heads)], 1)
    crossed = jnp.concatenate(
        [
            jnp.concatenate([r_rest[s, :half, :HDA] for s in range(heads)], 1),
            jnp.concatenate([r_rest[s, :half, HDA:] for s in range(heads)], 1),
        ],
        0,
    )
    audio_joined = jnp.concatenate([r_rest[s, half:, :] for s in range(heads)], 1)
    width = ws.shape[1] // chunks
    audio_width = wa.shape[1]

    def piece(ref, c):
        return ref if c == 0 else ref.at[:, (c - 1) * width : c * width]

    def rows_of(ref, c, block):
        size = part_few if c == 0 else part_rows
        return piece(ref.at[pl.ds(pl.multiple_of(block * size, size), size)], c)

    def first_hop(c):
        source, middle = (sum_a, mid_a) if c == 0 else (sum_v, mid_v)
        for d in range(1, n):
            copy = remote(
                rows_of(source, c, lax.rem(w + d, n)), piece(middle.at[w], c),
                d_send.at[c, d], d_recv.at[c, d], place(d, 0),
            )
            copy.start()
            d_copies[c, d] = copy

    def second_hop(c, d):
        source, middle, out = (sum_a, mid_a, out_a) if c == 0 else (sum_v, mid_v, out_v)
        origin = lax.rem(w + n - d, n)
        ready = piece(middle.at[origin], c) if d else rows_of(source, c, w)
        target = rows_of(out, c, h)
        away = remote(
            ready, target, e_send.at[c, d], e_recv.at[c, lax.rem(origin + n - h, n)],
            {"wide": w, "heads": origin},
        )
        here = pltpu.make_async_copy(ready, target, local.at[7 + c])

        @pl.when(origin != h)
        def _():
            away.start()

        @pl.when(origin == h)
        def _():
            here.start()

        last.append((origin, away, here))

    d_copies, last = {}, []
    order = list(range(1, chunks + 1)) + [0]
    for c in order:
        if c:
            cols = slice((c - 1) * width, c * width)
            sums = jnp.dot(
                joined, ws_all[:, :, cols].reshape(-1, width), preferred_element_type=jnp.float32
            ) + jnp.dot(
                crossed, wc_all[:, :, cols].reshape(-1, width), preferred_element_type=jnp.float32
            )
            sum_v[:, cols] = sums.astype(jnp.bfloat16)
        else:
            settle_weights(2)
            sums = jnp.dot(
                audio_joined, wa_all[...].reshape(-1, audio_width),
                preferred_element_type=jnp.float32,
            )
            sum_a[...] = sums.astype(jnp.bfloat16)
        first_hop(c)
        second_hop(c, 0)
    for c in order:
        for d in range(1, n):
            d_copies[c, d].wait_recv()
            second_hop(c, d)

    for origin, away, here in last:
        @pl.when(origin != h)
        def _():
            away.wait_send()

        @pl.when(origin == h)
        def _():
            here.wait()

    for c in order:
        out = out_a if c == 0 else out_v
        for d in range(1, n):
            who = lax.rem(h + d, n)
            target = rows_of(out, c, who)
            remote(
                target, target, e_send.at[c, 0], e_recv.at[c, n - d],
                {"wide": w, "heads": who},
            ).wait_recv()

    for copy in (
        list(a_copies.values()) + sum(w_copies, []) + sum(f_copies, [])
        + list(x_copies.values()) + list(d_copies.values())
    ):
        copy.wait_send()
    for step in range(steps):
        for way in (1, -1):
            @pl.when(sends(step, way))
            def _():
                for kind in range(2):
                    for d in range(n):
                        along(kind, d, step, way).wait_send()


def shards(*args):
    n = lax.axis_size("wide")
    count = lax.axis_size("heads")
    head_count = args[2].shape[1] // HDV
    if not (n == count == head_count and n % 2 == 0 and args[5].shape[0] % (16 * n) == 0):
        return general_shards(*args)
    (video_hidden, audio_hidden, vq, vk, vv, aq, ak, av, cvq, cak, cav, caq, cvk, cvv,
     vso, vco, aso, aco, table) = args
    rows, few = vq.shape[0], aq.shape[0]
    depth = rows + rows // 2 + 3 * few
    vmem = pl.BlockSpec(memory_space=pltpu.VMEM)
    anywhere = pl.BlockSpec(memory_space=pl.ANY)
    bf16 = jnp.bfloat16
    pack, wa, bias_v, bias_a = pl.pallas_call(
        functools.partial(pack_kernel, n),
        out_shape=(
            jax.ShapeDtypeStruct((n, depth, 2 * HDA), bf16),
            jax.ShapeDtypeStruct((2 * aso.shape[0], aso.shape[1]), bf16),
            jax.ShapeDtypeStruct((n, n * few), jnp.float32),
            jax.ShapeDtypeStruct((n, n * rows), jnp.float32),
        ),
        in_specs=[vmem] * 11 + [pl.BlockSpec(memory_space=pltpu.SMEM)],
        out_specs=(vmem, vmem, vmem, vmem),
        name="pack",
    )(cvq, cvk, cvv, aq, ak, av, caq, cak, cav, aso, aco, table)
    chunks = max(1, vso.shape[1] // 512)
    rest = rows // 2 + few
    dma = pltpu.SemaphoreType.DMA
    video_sum, audio_sum = pl.pallas_call(
        functools.partial(fused_kernel, n, chunks),
        out_shape=(
            jax.ShapeDtypeStruct(video_hidden.shape, bf16),
            jax.ShapeDtypeStruct(audio_hidden.shape, bf16),
        ),
        in_specs=[anywhere] * 7 + [vmem] * 2,
        out_specs=(anywhere, anywhere),
        scratch_shapes=[
            pltpu.VMEM((n, rows, HDV), bf16),
            pltpu.VMEM((n, rows, HDV), bf16),
            pltpu.VMEM((n, rows, HDV), bf16),
            pltpu.VMEM((n, depth, 2 * HDA), bf16),
            pltpu.VMEM((n,) + vso.shape, bf16),
            pltpu.VMEM((n,) + vco.shape, bf16),
            pltpu.VMEM((n,) + wa.shape, bf16),
            pltpu.VMEM((n, rows, HDV), bf16),
            pltpu.VMEM((n, rest, 2 * HDA), bf16),
            pltpu.VMEM((n * n, rows, HDV), bf16),
            pltpu.VMEM((n * n, rest, 2 * HDA), bf16),
            pltpu.VMEM(video_hidden.shape, bf16),
            pltpu.VMEM(audio_hidden.shape, bf16),
            pltpu.VMEM((n, rows // n, video_hidden.shape[1]), bf16),
            pltpu.VMEM((n, few // n, audio_hidden.shape[1]), bf16),
            dma((4, n)), dma((4, n)),
            dma((3, n)), dma((3, n)),
            dma((3, n)), dma((3, n)),
            dma((2, n)), dma((2, n)),
            dma((4 * n * (n - 1),)), dma((4 * n * (n - 1),)),
            dma((1 + chunks, n)), dma((1 + chunks, n)),
            dma((1 + chunks, n)), dma((1 + chunks, n)),
            dma((8 + chunks,)),
        ],
        compiler_params=pltpu.CompilerParams(collective_id=0, has_side_effects=True),
        name="joint",
    )(vq, vk, vv, pack, vso, vco, wa, bias_v, bias_a)
    video_out = video_hidden.astype(jnp.float32) + video_sum.astype(jnp.float32)
    audio_out = audio_hidden.astype(jnp.float32) + audio_sum.astype(jnp.float32)
    return (video_out.astype(bf16), audio_out.astype(bf16))


def solution(mesh):
    placed = (
        P(("groups", "wide"), "heads"),
        P(("groups", "wide"), "heads"),
        P(("groups", "wide"), "heads"),
        P(("groups", "wide"), "heads"),
        P(("groups", "wide"), "heads"),
        P(("groups", "wide"), "heads"),
        P(("groups", "wide"), "heads"),
        P(("groups", "wide"), "heads"),
        P(("groups", "wide"), "heads"),
        P(("groups", "wide"), "heads"),
        P(("groups", "wide"), "heads"),
        P(("groups", "wide"), "heads"),
        P(("groups", "wide"), "heads"),
        P(("groups", "wide"), "heads"),
        P("heads", "wide"),
        P("heads", "wide"),
        P("heads", "wide"),
        P("heads", "wide"),
        P("groups", None),
    )
    return jax.shard_map(
        shards,
        mesh=mesh,
        in_specs=placed,
        out_specs=(P(("groups", "wide"), "heads"), P(("groups", "wide"), "heads")),
        check_vma=False,
    )
```

profile of v0, /device:TPU:1, one launch (start us, length us, event | category | flops | bytes accessed | tf_op | source)
XLA Modules:
  0.0 92.9 jit_solution(11698880009314394108)
XLA Ops:
  0.6 2.5 %pack.1 = (bf16[4,576,128]{2,1,0:T(8,128)(2,1)}, bf16[512,512]{1,0:T(8,128)(2,1)}, f32[4,256]{1,0:T(4,128)}, f32[4,1024]{1,0:T(4,128)}) custom-call(bf16[256,256]{1,0:T(8,128)(2,1)} %cvq.1, bf16[256,256]{1,0:T(8,128)(2,1)} %cvk.1, bf16[256,256]{1,0:T(8,128)(2,1)} %cvv.1, bf16[64,256]{1,0:T(8,128)(2,1)} %aq.1, bf16[64,256]{1,0:T(8,128)(2,1)} %ak.1, ...), custom_call_target="tpu_custom_call" | custom-call | tf_op jit(solution)/shard_map/pack/pallas_call | solution.py:567
  3.2 0.0 copy-start
  3.2 87.0 %joint.1 = (bf16[256,1024]{1,0:T(8,128)(2,1)}, bf16[64,512]{1,0:T(8,128)(2,1)}) custom-call(bf16[256,512]{1,0:T(8,128)(2,1)} %vq.1, bf16[256,512]{1,0:T(8,128)(2,1)} %vk.1, bf16[256,512]{1,0:T(8,128)(2,1)} %vv.1, bf16[4,576,128]{2,1,0:T(8,128)(2,1)} %get-tuple-element.8.pack, bf16[512,1024]{1,0:T(8,128)(2,1)} %ws.1, bf16[256,1024]{1,0:T(8,128)(2,1)} %wc.1, ...), custom_call_target="tpu_custom_call" | custom-call | tf_op jit(solution)/shard_map/joint/pallas_call | solution.py:582
  90.2 0.0 copy-done
  90.2 0.0 copy-start.1
  90.2 0.0 copy-start.2
  90.2 2.1 %add_convert_fusion = bf16[256,1024]{1,0:T(8,128)(2,1)} fusion(bf16[256,1024]{1,0:T(8,128)(2,1)} %get-tuple-element.12, bf16[256,1024]{1,0:T(8,128)(2,1)S(1)} %copy-done), kind=kLoop, calls=%fused_computation | loop fusion | flops 1048576 | bytes 1572864 | tf_op jit(solution)/shard_map/convert_element_type | solution.py:620
  92.3 0.0 copy-done.1
  92.3 0.0 copy-done.2
  92.3 0.6 add_convert_fusion.1
Async XLA Ops:
  3.2 87.0 %copy-start = (bf16[256,1024]{1,0:T(8,128)(2,1)S(1)}, bf16[256,1024]{1,0:T(8,128)(2,1)}, u32[]{:S(2)}) copy-start(bf16[256,1024]{1,0:T(8,128)(2,1)} %param.19) | copy-start | bytes 1572868
  90.2 2.1 %copy-start.1 = (bf16[64,512]{1,0:T(8,128)(2,1)S(1)}, bf16[64,512]{1,0:T(8,128)(2,1)}, u32[]{:S(2)}) copy-start(bf16[64,512]{1,0:T(8,128)(2,1)} %param.20) | copy-start | bytes 196612
  90.2 2.1 %copy-start.2 = (bf16[64,512]{1,0:T(8,128)(2,1)S(1)}, bf16[64,512]{1,0:T(8,128)(2,1)}, u32[]{:S(2)}) copy-start(bf16[64,512]{1,0:T(8,128)(2,1)} %get-tuple-element.13) | copy-start | bytes 196612
where the time goes:
time: 93.2 us; the launch traced here: 92.9 us
  Pallas kernels  89.5 us (96%)
  other arithmetic  2.71 us (3%)
    pallas_call x1, Pallas kernels, shards(): pl.pallas_call(functools.partial(fused_kernel, n, chunks), out_shape=(jax...  87 us
    convert_element_type x2, other arithmetic, shards(): return (video_out.astype(bf16), audio_out.astype(bf16))  2.71 us
    pallas_call x1, Pallas kernels, shards(): pl.pallas_call(functools.partial(pack_kernel, n), out_shape=(jax.ShapeDty...  2.52 us

commit v1 on v0

v1 whole, which is shorter than its diff:
```python
import contextlib
import functools
import math

import jax
import jax.numpy as jnp
from jax import lax
from jax.experimental import pallas as pl
from jax.experimental.pallas import tpu as pltpu
from jax.sharding import PartitionSpec as P

HDV = 128
HDA = 64
REACH = 2


def passed_along(value, axis, by):
    length = lax.axis_size(axis)
    pairs = [(i, i + by) for i in range(length) if 0 <= i + by < length]
    return lax.ppermute(value, axis, pairs)


def empty_state(row_count, head_count, head_size):
    return (
        jnp.full((head_count, row_count), -1e30, jnp.float32),
        jnp.zeros((head_count, row_count), jnp.float32),
        jnp.zeros((head_count, row_count, head_size), jnp.float32),
    )


def absorb(state, queries, key_rows, value_rows, head_size, allowed):
    maxima, totals, running = state
    head_count = queries.shape[1] // head_size
    query_heads = queries.reshape(queries.shape[0], head_count, head_size)
    key_heads = key_rows.reshape(key_rows.shape[0], head_count, head_size)
    value_heads = value_rows.reshape(value_rows.shape[0], head_count, head_size)
    scores = jnp.einsum(
        "qhd,khd->hqk", query_heads, key_heads, preferred_element_type=jnp.float32
    ) * (1.0 / math.sqrt(head_size))
    if allowed is not None:
        scores = jnp.where(allowed[None, None, :], scores, -1e30)
    new_peak = jnp.maximum(maxima, jnp.max(scores, axis=2))
    weights = jnp.exp(scores - new_peak[:, :, None])
    if allowed is not None:
        weights = jnp.where(allowed[None, None, :], weights, 0.0)
    rescale = jnp.exp(maxima - new_peak)
    totals = totals * rescale + jnp.sum(weights, axis=2)
    running = running * rescale[:, :, None] + jnp.einsum(
        "hqk,khd->hqd",
        weights.astype(jnp.bfloat16),
        value_heads,
        preferred_element_type=jnp.float32,
    )
    return (new_peak, totals, running)


def finish(state, head_size):
    maxima, totals, running = state
    result = running / totals[:, :, None]
    return (
        result.transpose(1, 0, 2)
        .reshape(result.shape[1], result.shape[0] * head_size)
        .astype(jnp.bfloat16)
    )


def permitted(key_blocks, position, table_row, wide_count):
    offsets = key_blocks - position + REACH
    matches = (offsets[:, None] == jnp.arange(2 * REACH + 1, dtype=jnp.int32)[None, :]) & (
        table_row[None, :] > 0
    )
    inside = (key_blocks >= 0) & (key_blocks < wide_count)
    return jnp.any(matches, axis=1) & inside


def general_shards(
    video_hidden,
    audio_hidden,
    video_query,
    video_key,
    video_value,
    audio_query,
    audio_key,
    audio_value,
    cross_video_query,
    cross_audio_key,
    cross_audio_value,
    cross_audio_query,
    cross_video_key,
    cross_video_value,
    video_self_out,
    video_cross_out,
    audio_self_out,
    audio_cross_out,
    intersection,
):
    position = lax.axis_index("wide")
    wide_count = lax.axis_size("wide")
    video_count = video_query.shape[0]
    audio_count = audio_query.shape[0]
    head_count = video_query.shape[1] // HDV
    video_start = empty_state(video_count, head_count, HDV)
    audio_start = empty_state(audio_count, head_count, HDA)
    carried = (video_start, audio_start)
    portion = (
        lax.all_gather(video_key, "wide", axis=0, tiled=True),
        lax.all_gather(video_value, "wide", axis=0, tiled=True),
        lax.all_gather(audio_key, "wide", axis=0, tiled=True),
        lax.all_gather(audio_value, "wide", axis=0, tiled=True),
    )
    video_state = absorb(carried[0], video_query, portion[0], portion[1], HDV, None)
    audio_state = absorb(carried[1], audio_query, portion[2], portion[3], HDA, None)
    table_row = lax.dynamic_slice_in_dim(intersection, position, 1, 0)[0]
    padded_table = jnp.pad(intersection, ((REACH, REACH), (0, 0)))
    flag_row = jnp.diagonal(
        jnp.fliplr(lax.dynamic_slice_in_dim(padded_table, position, 2 * REACH + 1, 0))
    )
    stacked = jnp.concatenate(
        [cross_audio_key, cross_audio_value, cross_video_key, cross_video_value], 0
    )

    def take_cross(carried, portion, block):
        audio_keys = portion[:audio_count]
        audio_values = portion[audio_count : 2 * audio_count]
        video_keys = portion[2 * audio_count : 2 * audio_count + video_count]
        video_values = portion[2 * audio_count + video_count :]
        audio_blocks = jnp.full((audio_count,), block, jnp.int32)
        video_blocks = jnp.full((video_count,), block, jnp.int32)
        return (
            absorb(
                carried[0],
                cross_video_query,
                audio_keys,
                audio_values,
                HDA,
                permitted(audio_blocks, position, table_row, wide_count),
            ),
            absorb(
                carried[1],
                cross_audio_query,
                video_keys,
                video_values,
                HDA,
                permitted(video_blocks, position, flag_row, wide_count),
            ),
        )

    cross_start = (
        empty_state(video_count, head_count, HDA),
        empty_state(audio_count, head_count, HDA),
    )
    carried = take_cross(cross_start, stacked, position)
    for offset in range(-REACH, REACH + 1):
        if offset != 0:
            nearby = passed_along(stacked, "wide", -offset)
            carried = take_cross(carried, nearby, position + offset)
    to_video, to_audio = carried
    video_joined = jnp.concatenate([finish(video_state, HDV), finish(to_video, HDA)], 1)
    audio_joined = jnp.concatenate([finish(audio_state, HDA), finish(to_audio, HDA)], 1)
    video_weights = jnp.concatenate([video_self_out, video_cross_out], 0)
    audio_weights = jnp.concatenate([audio_self_out, audio_cross_out], 0)
    video_terms = jnp.dot(
        video_joined,
        lax.all_gather(video_weights, "wide", axis=1, tiled=True),
        preferred_element_type=jnp.float32,
    )
    audio_terms = jnp.dot(
        audio_joined,
        lax.all_gather(audio_weights, "wide", axis=1, tiled=True),
        preferred_element_type=jnp.float32,
    )
    video_sum, audio_sum = (
        lax.psum_scatter(
            video_terms.astype(jnp.bfloat16), "heads", scatter_dimension=1, tiled=True
        ).astype(jnp.float32),
        lax.psum_scatter(
            audio_terms.astype(jnp.bfloat16), "heads", scatter_dimension=1, tiled=True
        ).astype(jnp.float32),
    )
    video_out = (video_hidden.astype(jnp.float32) + video_sum).astype(jnp.bfloat16)
    audio_out = (audio_hidden.astype(jnp.float32) + audio_sum).astype(jnp.bfloat16)
    return (video_out, audio_out)


NT = (((1,), (1,)), ((), ()))
MESH = pl.DeviceIdType.MESH


def scope(name):
    return contextlib.nullcontext()


def softmax(scores, head_size):
    factor = math.log2(math.e) / math.sqrt(head_size)
    weights = jnp.exp2((scores - jnp.max(scores, axis=1, keepdims=True)) * factor)
    return weights.astype(jnp.bfloat16), jnp.sum(weights, axis=1, keepdims=True)


def scored(queries, keys):
    return lax.dot_general(queries, keys, NT, preferred_element_type=jnp.float32)


def mixed(weights, values):
    return jnp.dot(weights, values, preferred_element_type=jnp.float32)


def joint_kernel(
    n,
    vq, vk, vv, cvq, cvk, cvv, aq, ak, av, caq, cak, cav, ws, wc, aso, aco, table,
    out_v, out_a,
    q_all, k_all, v_all, wide_stage, few_stage, pack, p_all, ws_all, wc_all, wa_all,
    tall_bias, wide_bias, o_self, o_rest, r_self, r_rest, totals, sum_v, sum_a, mid_v, mid_a,
    a_send, a_recv, w_send, w_recv, f_send, f_recv, x_send, x_recv, z_send, z_recv, r_send,
    d_send, d_recv, e_send, e_recv, local,
):
    w = lax.axis_index("wide")
    h = lax.axis_index("heads")
    rows, few = vq.shape[0], aq.shape[0]
    half = rows // 2
    part_rows, part_few = rows // n, few // n
    depth = p_all.shape[1]
    bf16 = jnp.bfloat16

    def place(dw, dh):
        return {"wide": lax.rem(w + dw, n), "heads": lax.rem(h + dh, n)}

    def remote(source, target, send, recv, device):
        return pltpu.make_async_remote_copy(
            src_ref=source, dst_ref=target, send_sem=send, recv_sem=recv,
            device_id=device, device_id_type=MESH,
        )

    others = [(d, 0) for d in range(1, n)] + [(0, d) for d in range(1, n)]
    barrier = pltpu.get_barrier_semaphore()
    for dw, dh in others:
        pl.semaphore_signal(barrier, inc=1, device_id=place(dw, dh), device_id_type=MESH)

    def head_cols(ref, who):
        return ref.at[:, pl.ds(pl.multiple_of(who * HDV, HDV), HDV)]

    def start(copies):
        for copy in copies:
            copy.start()
        return copies

    staged = start(
        [
            pltpu.make_async_copy(source, wide_stage.at[i], local.at[i])
            for i, source in enumerate((cvq, cvk, cvv))
        ]
        + [
            pltpu.make_async_copy(source, few_stage.at[i], local.at[3 + i])
            for i, source in enumerate((cak, caq, av, aq, cav, ak))
        ]
    )
    own = start(
        [
            pltpu.make_async_copy(head_cols(source, w), target.at[w], local.at[9 + i])
            for i, (source, target) in enumerate(((vq, q_all), (vk, k_all), (vv, v_all)))
        ]
        + [
            pltpu.make_async_copy(source, target.at[h], local.at[12 + i])
            for i, (source, target) in enumerate(((ws, ws_all), (wc, wc_all)))
        ]
    )
    for j in range(n):
        for k, source in enumerate((aso, aco)):
            at = (2 * j + k) * HDA
            pltpu.make_async_copy(
                source.at[j * HDA : (j + 1) * HDA], wa_all.at[h, at : at + HDA], local.at[14]
            ).start()
    own.append(pltpu.make_async_copy(wa_all.at[h], wa_all.at[h], local.at[14]))
    with scope("T0barrier"):
        pl.semaphore_wait(barrier, len(others))

    a_copies, sent = {}, []

    def exchange(i, d, source, target):
        copy = remote(source, target, a_send.at[i, d], a_recv.at[i, d], place(d, 0))
        copy.start()
        a_copies[i, d] = copy

    for i, (source, target) in enumerate(((vq, q_all), (vk, k_all), (vv, v_all))):
        for d in range(1, n):
            exchange(i, d, head_cols(source, lax.rem(w + d, n)), target.at[w])

    targets = (ws_all, wc_all, wa_all)
    sources = (ws, wc, wa_all.at[h])
    partner = {"wide": w, "heads": h + 1 - 2 * lax.rem(h, 2)}
    w_copies, f_copies = {}, {i: [] for i in range(3)}

    def send_weights(i):
        for k in range(1, n // 2):
            copy = remote(
                sources[i], targets[i].at[h], w_send.at[i, k], w_recv.at[i, k], place(0, 2 * k)
            )
            copy.start()
            w_copies[i, k] = copy

    def share_weights(i):
        copy = remote(sources[i], targets[i].at[h], f_send.at[i, 0], f_recv.at[i, 0], partner)
        copy.start()
        f_copies[i].append(copy)

    def pass_weights(i):
        for k in range(1, n // 2):
            w_copies[i, k].wait_recv()
            slot = targets[i].at[lax.rem(h + n - 2 * k, n)]
            copy = remote(slot, slot, f_send.at[i, k], f_recv.at[i, k], partner)
            copy.start()
            f_copies[i].append(copy)

    def settle_weights(i):
        for copy in f_copies[i]:
            copy.wait_recv()

    send_weights(0)
    share_weights(0)
    share_weights(1)

    for copy in staged:
        copy.wait()
    for j in range(n):
        cols = slice(j * HDA, (j + 1) * HDA)
        pack[j, :rows, :] = jnp.concatenate([wide_stage[0, :, cols], wide_stage[1, :, cols]], 1)
        pack[j, rows : rows + half, :] = jnp.concatenate(
            [wide_stage[2, :half, cols], wide_stage[2, half:, cols]], 1
        )
        for k in range(3):
            at = rows + half + k * few
            pack[j, at : at + few, :] = jnp.concatenate(
                [few_stage[2 * k, :, cols], few_stage[2 * k + 1, :, cols]], 1
            )
    for d in range(1, n):
        exchange(3, d, pack.at[lax.rem(w + d, n)], p_all.at[w])
    own_pack = pltpu.make_async_copy(pack.at[w], p_all.at[w], local.at[0])
    own_pack.start()
    own.pop().wait()
    share_weights(2)

    for i in range(n):
        for j in range(n):
            column = j - i + REACH
            drop = jnp.float32(-1e30)
            if 0 <= column < table.shape[1]:
                drop = jnp.where(table[i, column] > 0, jnp.float32(0.0), drop)
            tall_bias[i * part_rows : (i + 1) * part_rows, j * few : (j + 1) * few] = jnp.full(
                (part_rows, few), drop
            )
            wide_bias[j * few : (j + 1) * few, i * rows : (i + 1) * rows] = jnp.full(
                (few, rows), drop
            )

    mine = h * n + w
    side = w // (n // 2)
    mate = w + 1 - 2 * lax.rem(w, 2)
    across_side = n // 2 - side
    far_start = (1 - side) * (n // 2)
    inner = (w > 0) & (w < n - 1)
    splits = (part_few * n + half // 2, half // 2)
    starts = (0, splits[0])
    x_copies = {}

    def chunk(ref, kind):
        if kind == 0:
            return ref
        return ref.at[pl.ds(starts[kind - 1], splits[kind - 1])]

    def buffers(kind):
        return (o_self, r_self) if kind == 0 else (o_rest, r_rest)

    def across(kind, d):
        source, landing = buffers(kind)
        copy = remote(
            source.at[lax.rem(h + d, n)], landing.at[mine],
            x_send.at[kind, d], x_recv.at[kind, d], place(0, d),
        )
        copy.start()
        x_copies[kind, d] = copy

    def along(kind, d):
        source, landing = buffers(kind)
        slot = lax.rem(h + n - d, n) * n + w
        piece = chunk(source.at[h] if d == 0 else landing.at[slot], kind)
        where = chunk(landing.at[slot], kind)
        for k, device, role in ((0, mate, 0), (1, across_side, 1 + lax.rem(w, 2))):
            copy = remote(
                piece, where, z_send.at[kind, d, k], z_recv.at[kind, d, role],
                {"wide": device, "heads": h},
            )
            copy.start()
            sent.append(copy)

    def arrival(kind, d, k):
        landing = buffers(kind)[1]
        slot = lax.rem(h + n - d, n) * n + far_start + k
        where = chunk(landing.at[slot], kind)
        return remote(
            where, where, r_send.at[kind, d, k], z_recv.at[kind, d, 1 + k],
            {"wide": mate, "heads": h},
        )

    def forward(kind, d):
        for k in range(2):
            copy = arrival(kind, d, k)
            copy.wait_recv()

            @pl.when(inner)
            def _():
                copy.start()

    def from_mate(kind, d):
        landing = buffers(kind)[1]
        slot = lax.rem(h + n - d, n) * n + mate
        where = chunk(landing.at[slot], kind)
        remote(
            where, where, z_send.at[kind, d, 0], z_recv.at[kind, d, 0],
            {"wide": mate, "heads": h},
        ).wait_recv()

    with scope("T1self"):
        for copy in own[:3]:
            copy.wait()
        for i in range(3):
            for d in range(1, n):
                a_copies[i, d].wait_recv()
    keys = k_all[...].reshape(n * rows, HDV)
    values = v_all[...].reshape(n * rows, HDV)

    def self_scores(d):
        at = pl.multiple_of(lax.rem(h + d, n) * part_rows, part_rows)
        return scored(q_all[:, pl.ds(at, part_rows), :].reshape(rows, HDV), keys)

    scores = self_scores(0)
    for d in range(n):
        following = self_scores(d + 1) if d + 1 < n else None
        weights, sums = softmax(scores, HDV)
        result = (mixed(weights, values) / sums).astype(bf16)
        scores = following
        o_self[pl.ds(lax.rem(h + d, n), 1)] = result[None]
        if d:
            across(0, d)
        else:
            r_self[pl.ds(mine, 1)] = result[None]
            along(0, 0)
        if d > 1:
            x_copies[0, d - 1].wait_recv()
            along(0, d - 1)
    send_weights(1)
    with scope("T2x"):
        x_copies[0, n - 1].wait_recv()
    along(0, n - 1)

    with scope("T3rest"):
        own_pack.wait()
        for d in range(1, n):
            a_copies[3, d].wait_recv()
    at = rows + half
    lane = lax.broadcasted_iota(jnp.int32, (n * few, 2 * HDA), 1)
    left = lane < HDA
    both = p_all[:, :rows, :].reshape(n * rows, 2 * HDA)
    vals = p_all[:, rows:at, :].reshape(n * half, 2 * HDA)
    keyed = p_all[:, at : at + few, :].reshape(n * few, 2 * HDA)
    asked = p_all[:, at + few : at + 2 * few, :].reshape(n * few, 2 * HDA)
    third = p_all[:, at + 2 * few : depth, :].reshape(n * few, 2 * HDA)
    zero = jnp.zeros_like(keyed)
    key_left = jnp.where(left, keyed, zero)
    query_right = jnp.where(left, zero, keyed)
    key_right = jnp.where(left, zero, third)
    twice = jnp.concatenate([third[:, :HDA], third[:, :HDA]], 1)

    scores_a = scored(asked, key_right)
    scores_c = scored(query_right, both) + wide_bias[...]
    weights, sums = softmax(scores_a, HDA)
    audio_own = mixed(weights, asked) / sums
    weights, sums = softmax(scores_c, HDA)
    upper = jnp.concatenate([weights[:, j * rows : j * rows + half] for j in range(n)], 1)
    lower = jnp.concatenate([weights[:, j * rows + half : (j + 1) * rows] for j in range(n)], 1)
    audio_other = (pltpu.roll(mixed(upper, vals), HDA, 1) + mixed(lower, vals)) / sums
    audio = jnp.where(left, audio_own, audio_other).astype(bf16)
    for t in range(n):
        o_rest[t, : n * part_few, :] = jnp.concatenate(
            [audio[j * few + t * part_few : j * few + (t + 1) * part_few, :] for j in range(n)], 0
        )
    forward(0, 0)

    def cross_scores(d):
        begin = pl.multiple_of(lax.rem(h + d, n) * part_rows, part_rows)
        queries = p_all[:, pl.ds(begin, part_rows), :].reshape(rows, 2 * HDA)
        return scored(queries, key_left) + tall_bias[...]

    low = lax.broadcasted_iota(jnp.int32, (half, 2 * HDA), 1) < HDA
    scores = cross_scores(0)
    for d in range(n):
        following = cross_scores(d + 1) if d + 1 < n else None
        weights, sums = softmax(scores, HDA)
        result = mixed(weights, twice) / sums
        scores = following
        block = lax.rem(h + d, n)
        packed = jnp.where(low, result[:half], result[half:]).astype(bf16)
        o_rest[pl.ds(block, 1), n * part_few :, :] = packed[None]
        if d:
            across(1, d)
            forward(0, d)
        else:
            r_rest[pl.ds(mine, 1)] = o_rest[pl.ds(h, 1)]
            along(1, 0)
            along(2, 0)
        if d > 1:
            x_copies[1, d - 1].wait_recv()
            along(1, d - 1)
            along(2, d - 1)
    send_weights(2)
    with scope("T4x"):
        x_copies[1, n - 1].wait_recv()
    along(1, n - 1)
    along(2, n - 1)

    with scope("T5w"):
        own[3].wait()
        own[4].wait()
        pass_weights(0)
        settle_weights(0)
    with scope("T6self"):
        for d in range(n):
            from_mate(0, d)
    heads = n * n
    joined = jnp.concatenate([r_self[s] for s in range(heads)], 1)
    totals[...] = jnp.dot(
        joined, ws_all[...].reshape(-1, ws.shape[1]), preferred_element_type=jnp.float32
    )
    with scope("T7w"):
        pass_weights(1)
        settle_weights(1)
        pass_weights(2)
        settle_weights(2)

    chunks = d_send.shape[0] - 1
    width = ws.shape[1] // chunks
    d_copies, last = {}, []

    def cut(ref, c):
        return ref if c == 0 else ref.at[:, (c - 1) * width : c * width]

    def rows_of(ref, c, block):
        size = part_few if c == 0 else part_rows
        return cut(ref.at[pl.ds(pl.multiple_of(block * size, size), size)], c)

    def first_hop(c, b):
        source, middle = (sum_a, mid_a) if c == 0 else (sum_v, mid_v)

        @pl.when(w != b)
        def _():
            remote(
                rows_of(source, c, b), cut(middle.at[w], c),
                d_send.at[c, b], d_recv.at[c, w], {"wide": b, "heads": h},
            ).start()

    def second_hop(c, origin):
        source, middle, out = (sum_a, mid_a, out_a) if c == 0 else (sum_v, mid_v, out_v)

        def go(ready):
            target = rows_of(out, c, h)

            @pl.when(origin != h)
            def _():
                remote(
                    ready, target, e_send.at[c, origin], e_recv.at[c, h],
                    {"wide": w, "heads": origin},
                ).start()

            @pl.when(origin == h)
            def _():
                pltpu.make_async_copy(ready, target, e_send.at[c, origin]).start()

        @pl.when(w == origin)
        def _():
            go(rows_of(source, c, w))

        @pl.when(w != origin)
        def _():
            piece = cut(middle.at[origin], c)
            remote(
                piece, piece, d_send.at[c, origin], d_recv.at[c, origin],
                {"wide": origin, "heads": h},
            ).wait_recv()
            go(piece)

    flat_c = wc_all[...].reshape(-1, wc.shape[1])
    for u in range(2):
        with scope("T8gather%d" % u):
            for d in range(n):
                forward(1 + u, d)
            for d in range(n):
                from_mate(1 + u, d)
        begin = n * part_few + u * (half // 2)
        piece = slice(begin, begin + half // 2)
        crossed = jnp.concatenate(
            [
                jnp.concatenate([r_rest[s, piece, :HDA] for s in range(heads)], 1),
                jnp.concatenate([r_rest[s, piece, HDA:] for s in range(heads)], 1),
            ],
            0,
        )
        products = jnp.dot(crossed, flat_c, preferred_element_type=jnp.float32)
        size = half // 2
        for k in range(2):
            where = slice((u + 2 * k) * size, (u + 2 * k + 1) * size)
            sum_v[where, :] = (
                totals[where, :] + products[k * size : (k + 1) * size, :]
            ).astype(bf16)
        for c in range(1, chunks + 1):
            for k in (1 - u, u):
                first_hop(c, u + 2 * k)
        if u == 0:
            audio_joined = jnp.concatenate([r_rest[s, : n * part_few, :] for s in range(heads)], 1)
            sum_a[...] = jnp.dot(
                audio_joined, wa_all[...].reshape(-1, aso.shape[1]),
                preferred_element_type=jnp.float32,
            ).astype(bf16)
            for b in range(n):
                first_hop(0, b)
    order = list(range(1, chunks + 1)) + [0]
    with scope("T9results"):
        for c in order:
            for origin in range(n):
                second_hop(c, origin)

    with scope("TAout"):
        for c in order:
            out = out_a if c == 0 else out_v
            for who in range(n):
                @pl.when(who != h)
                def _():
                    target = rows_of(out, c, who)
                    remote(
                        target, target, e_send.at[c, who], e_recv.at[c, who],
                        {"wide": w, "heads": who},
                    ).wait()

                @pl.when(who == h)
                def _():
                    target = rows_of(out, c, h)
                    pltpu.make_async_copy(target, target, e_send.at[c, who]).wait()

    with scope("TBsends"):
        for copy in (
            list(a_copies.values()) + list(w_copies.values()) + sum(f_copies.values(), [])
            + list(x_copies.values()) + sent
        ):
            copy.wait_send()
        for c in order:
            source = sum_a if c == 0 else sum_v
            for b in range(n):
                @pl.when(w != b)
                def _():
                    piece = rows_of(source, c, b)
                    remote(
                        piece, piece, d_send.at[c, b], d_recv.at[c, b], {"wide": b, "heads": h}
                    ).wait_send()

        @pl.when(inner)
        def _():
            for kind in range(3):
                for d in range(n):
                    for k in range(2):
                        arrival(kind, d, k).wait_send()


def shards(*args):
    n = lax.axis_size("wide")
    count = lax.axis_size("heads")
    head_count = args[2].shape[1] // HDV
    if not (n == count == head_count == 2 * REACH and args[5].shape[0] % (16 * n) == 0):
        return general_shards(*args)
    (video_hidden, audio_hidden, vq, vk, vv, aq, ak, av, cvq, cak, cav, caq, cvk, cvv,
     vso, vco, aso, aco, table) = args
    rows, few = vq.shape[0], aq.shape[0]
    depth = rows + rows // 2 + 3 * few
    anywhere = pl.BlockSpec(memory_space=pl.ANY)
    bf16, f32 = jnp.bfloat16, jnp.float32
    chunks = max(1, vso.shape[1] // 512)
    rest = rows // 2 + few
    dma = pltpu.SemaphoreType.DMA
    video_sum, audio_sum = pl.pallas_call(
        functools.partial(joint_kernel, n),
        out_shape=(
            jax.ShapeDtypeStruct(video_hidden.shape, bf16),
            jax.ShapeDtypeStruct(audio_hidden.shape, bf16),
        ),
        in_specs=[anywhere] * 16 + [pl.BlockSpec(memory_space=pltpu.SMEM)],
        out_specs=(anywhere, anywhere),
        scratch_shapes=[
            pltpu.VMEM((n, rows, HDV), bf16),
            pltpu.VMEM((n, rows, HDV), bf16),
            pltpu.VMEM((n, rows, HDV), bf16),
            pltpu.VMEM((3,) + cvq.shape, bf16),
            pltpu.VMEM((6,) + aq.shape, bf16),
            pltpu.VMEM((n, depth, 2 * HDA), bf16),
            pltpu.VMEM((n, depth, 2 * HDA), bf16),
            pltpu.VMEM((n,) + vso.shape, bf16),
            pltpu.VMEM((n,) + vco.shape, bf16),
            pltpu.VMEM((n, 2 * aso.shape[0], aso.shape[1]), bf16),
            pltpu.VMEM((rows, n * few), f32),
            pltpu.VMEM((n * few, n * rows), f32),
            pltpu.VMEM((n, rows, HDV), bf16),
            pltpu.VMEM((n, rest, 2 * HDA), bf16),
            pltpu.VMEM((n * n, rows, HDV), bf16),
            pltpu.VMEM((n * n, rest, 2 * HDA), bf16),
            pltpu.VMEM(video_hidden.shape, f32),
            pltpu.VMEM(video_hidden.shape, bf16),
            pltpu.VMEM(audio_hidden.shape, bf16),
            pltpu.VMEM((n, rows // n, video_hidden.shape[1]), bf16),
            pltpu.VMEM((n, few // n, audio_hidden.shape[1]), bf16),
            dma((4, n)), dma((4, n)),
            dma((3, n)), dma((3, n)),
            dma((3, n)), dma((3, n)),
            dma((2, n)), dma((2, n)),
            dma((3, n, 2)), dma((3, n, 3)), dma((3, n, 2)),
            dma((1 + chunks, n)), dma((1 + chunks, n)),
            dma((1 + chunks, n)), dma((1 + chunks, n)),
            dma((15,)),
        ],
        compiler_params=pltpu.CompilerParams(collective_id=0, has_side_effects=True),
        name="joint",
    )(vq, vk, vv, cvq, cvk, cvv, aq, ak, av, caq, cak, cav, vso, vco, aso, aco, table)
    video_out = video_hidden.astype(f32) + video_sum.astype(f32)
    audio_out = audio_hidden.astype(f32) + audio_sum.astype(f32)
    return (video_out.astype(bf16), audio_out.astype(bf16))


def solution(mesh):
    placed = (
        P(("groups", "wide"), "heads"),
        P(("groups", "wide"), "heads"),
        P(("groups", "wide"), "heads"),
        P(("groups", "wide"), "heads"),
        P(("groups", "wide"), "heads"),
        P(("groups", "wide"), "heads"),
        P(("groups", "wide"), "heads"),
        P(("groups", "wide"), "heads"),
        P(("groups", "wide"), "heads"),
        P(("groups", "wide"), "heads"),
        P(("groups", "wide"), "heads"),
        P(("groups", "wide"), "heads"),
        P(("groups", "wide"), "heads"),
        P(("groups", "wide"), "heads"),
        P("heads", "wide"),
        P("heads", "wide"),
        P("heads", "wide"),
        P("heads", "wide"),
        P("groups", None),
    )
    return jax.shard_map(
        shards,
        mesh=mesh,
        in_specs=placed,
        out_specs=(P(("groups", "wide"), "heads"), P(("groups", "wide"), "heads")),
        check_vma=False,
    )
```

time: 93.2 us -> 100 us (1.073)
  the two profiles are of different devices: /device:TPU:1 before, /device:TPU:29 now
where the time goes in v1:
time: 100 us
  Pallas kernels  96.8 us (97%)
  other arithmetic  2.71 us (3%)
    pallas_call x1, Pallas kernels, shards(): pl.pallas_call(functools.partial(joint_kernel, n), out_shape=(jax.ShapeDt...  96.8 us
    convert_element_type x2, other arithmetic, shards(): return (video_out.astype(bf16), audio_out.astype(bf16))  2.71 us

profile of v1, /device:TPU:29, one launch (start us, length us, event | category | flops | bytes accessed | tf_op | source)
XLA Modules:
  0.0 100.2 jit_solution(16958920010880719857)
XLA Ops:
  0.6 0.0 copy-start
  0.6 96.8 %joint.1 = (bf16[256,1024]{1,0:T(8,128)(2,1)}, bf16[64,512]{1,0:T(8,128)(2,1)}) custom-call(bf16[256,512]{1,0:T(8,128)(2,1)} %vq.1, bf16[256,512]{1,0:T(8,128)(2,1)} %vk.1, bf16[256,512]{1,0:T(8,128)(2,1)} %vv.1, bf16[256,256]{1,0:T(8,128)(2,1)} %cvq.1, bf16[256,256]{1,0:T(8,128)(2,1)} %cvk.1, bf16[256,256]{1,0:T(8,128)(2,1)} %cvv.1, bf16[64,256]{1,0:T(8,128)(2,1)} %aq.1, ...), custom_call_target="tpu_custom_call" | custom-call | tf_op jit(solution)/shard_map/joint/pallas_call | solution.py:685
  97.5 0.0 copy-done
  97.5 0.0 copy-start.1
  97.5 0.0 copy-start.2
  97.5 2.1 %add_convert_fusion = bf16[256,1024]{1,0:T(8,128)(2,1)} fusion(bf16[256,1024]{1,0:T(8,128)(2,1)} %get-tuple-element.4, bf16[256,1024]{1,0:T(8,128)(2,1)S(1)} %copy-done), kind=kLoop, calls=%fused_computation | loop fusion | flops 1048576 | bytes 1572864 | tf_op jit(solution)/shard_map/convert_element_type | solution.py:729
  99.6 0.0 copy-done.1
  99.6 0.0 copy-done.2
  99.6 0.6 add_convert_fusion.1
Async XLA Ops:
  0.6 96.8 %copy-start = (bf16[256,1024]{1,0:T(8,128)(2,1)S(1)}, bf16[256,1024]{1,0:T(8,128)(2,1)}, u32[]{:S(2)}) copy-start(bf16[256,1024]{1,0:T(8,128)(2,1)} %param.19) | copy-start | bytes 1572868
  97.5 2.1 %copy-start.1 = (bf16[64,512]{1,0:T(8,128)(2,1)S(1)}, bf16[64,512]{1,0:T(8,128)(2,1)}, u32[]{:S(2)}) copy-start(bf16[64,512]{1,0:T(8,128)(2,1)} %param.20) | copy-start | bytes 196612
  97.5 2.1 %copy-start.2 = (bf16[64,512]{1,0:T(8,128)(2,1)S(1)}, bf16[64,512]{1,0:T(8,128)(2,1)}, u32[]{:S(2)}) copy-start(bf16[64,512]{1,0:T(8,128)(2,1)} %get-tuple-element.5) | copy-start | bytes 196612

commit v2 on v1

--- a/solution.py
+++ b/solution.py
@@ -209,10 +209,11 @@
     vq, vk, vv, cvq, cvk, cvv, aq, ak, av, caq, cak, cav, ws, wc, aso, aco, table,
     out_v, out_a,
     q_all, k_all, v_all, wide_stage, few_stage, pack, p_all, ws_all, wc_all, wa_all,
-    tall_bias, wide_bias, o_self, o_rest, r_self, r_rest, totals, sum_v, sum_a, mid_v, mid_a,
-    a_send, a_recv, w_send, w_recv, f_send, f_recv, x_send, x_recv, z_send, z_recv, r_send,
-    d_send, d_recv, e_send, e_recv, local,
+    tall_bias, wide_bias, o_self, o_rest, r_self, r_rest, totals, sum_v, sum_a,
+    a_send, a_recv, w_send, w_recv, x_send, x_recv, z_send, z_recv, m_recv, r_send,
+    e_send, e_recv, local,
 ):
+    g = lax.axis_index("groups")
     w = lax.axis_index("wide")
     h = lax.axis_index("heads")
     rows, few = vq.shape[0], aq.shape[0]
@@ -221,6 +222,13 @@
     depth = p_all.shape[1]
     bf16 = jnp.bfloat16
 
+    mine = h * n + w
+    side = w // (n // 2)
+    mate = w + 1 - 2 * lax.rem(w, 2)
+    across_side = n // 2 - side
+    far_start = (1 - side) * (n // 2)
+    inner = (w > 0) & (w < n - 1)
+
     def place(dw, dh):
         return {"wide": lax.rem(w + dw, n), "heads": lax.rem(h + dh, n)}
 
@@ -234,6 +242,11 @@
     barrier = pltpu.get_barrier_semaphore()
     for dw, dh in others:
         pl.semaphore_signal(barrier, inc=1, device_id=place(dw, dh), device_id_type=MESH)
+    twin = {"groups": 1 - g}
+    pl.semaphore_signal(barrier, inc=1, device_id=twin, device_id_type=MESH)
+
+    def settle(piece, sem):
+        pltpu.make_async_copy(piece, piece, sem).wait()
 
     def head_cols(ref, who):
         return ref.at[:, pl.ds(pl.multiple_of(who * HDV, HDV), HDV)]
@@ -271,52 +284,57 @@
             ).start()
     own.append(pltpu.make_async_copy(wa_all.at[h], wa_all.at[h], local.at[14]))
     with scope("T0barrier"):
-        pl.semaphore_wait(barrier, len(others))
-
-    a_copies, sent = {}, []
-
-    def exchange(i, d, source, target):
-        copy = remote(source, target, a_send.at[i, d], a_recv.at[i, d], place(d, 0))
-        copy.start()
-        a_copies[i, d] = copy
-
-    for i, (source, target) in enumerate(((vq, q_all), (vk, k_all), (vv, v_all))):
-        for d in range(1, n):
-            exchange(i, d, head_cols(source, lax.rem(w + d, n)), target.at[w])
+        pl.semaphore_wait(barrier, len(others) + 1)
+
+    far_end = (1 - side) * (n - 1)
+
+    def exchange(target):
+        for i, (source, landing) in enumerate(((vq, q_all), (vk, k_all), (vv, v_all))):
+            remote(
+                head_cols(source, target), landing.at[w], a_send.at[i], a_recv.at[i],
+                {"wide": target, "heads": h},
+            ).start()
+
+    near = jnp.where(inner, across_side, mate)
+    last = jnp.where(inner, mate, across_side)
+    for target in (far_end, near, last):
+        exchange(target)
 
     targets = (ws_all, wc_all, wa_all)
     sources = (ws, wc, wa_all.at[h])
     partner = {"wide": w, "heads": h + 1 - 2 * lax.rem(h, 2)}
-    w_copies, f_copies = {}, {i: [] for i in range(3)}
+    opposite = lax.rem(h + n // 2, n)
+
+    def part_of(ref, which):
+        size = ref.shape[0] // 2
+        return ref.at[pl.ds(pl.multiple_of(which * size, size), size)]
 
     def send_weights(i):
-        for k in range(1, n // 2):
-            copy = remote(
-                sources[i], targets[i].at[h], w_send.at[i, k], w_recv.at[i, k], place(0, 2 * k)
-            )
-            copy.start()
-            w_copies[i, k] = copy
+        remote(
+            part_of(sources[i], g), part_of(targets[i].at[h], g),
+            w_send.at[i, 0], w_recv.at[i, 0], {"wide": w, "heads": opposite},
+        ).start()
 
     def share_weights(i):
-        copy = remote(sources[i], targets[i].at[h], f_send.at[i, 0], f_recv.at[i, 0], partner)
-        copy.start()
-        f_copies[i].append(copy)
+        remote(sources[i], targets[i].at[h], w_send.at[i, 1], w_recv.at[i, 1], partner).start()
+
+    def swap_weights(i):
+        piece = part_of(targets[i].at[opposite], g)
+        settle(piece, w_recv.at[i, 0])
+        remote(piece, piece, w_send.at[i, 2], w_recv.at[i, 2], twin).start()
 
     def pass_weights(i):
-        for k in range(1, n // 2):
-            w_copies[i, k].wait_recv()
-            slot = targets[i].at[lax.rem(h + n - 2 * k, n)]
-            copy = remote(slot, slot, f_send.at[i, k], f_recv.at[i, k], partner)
-            copy.start()
-            f_copies[i].append(copy)
+        slot = targets[i].at[opposite]
+        settle(part_of(slot, 1 - g), w_recv.at[i, 2])
+        remote(slot, slot, w_send.at[i, 3], w_recv.at[i, 3], partner).start()
 
     def settle_weights(i):
-        for copy in f_copies[i]:
-            copy.wait_recv()
-
-    send_weights(0)
-    share_weights(0)
-    share_weights(1)
+        settle(targets[i].at[h], w_recv.at[i, 1])
+        settle(targets[i].at[h], w_recv.at[i, 3])
+
+    for i in range(2):
+        send_weights(i)
+        share_weights(i)
 
     for copy in staged:
         copy.wait()
@@ -331,8 +349,18 @@
             pack[j, at : at + few, :] = jnp.concatenate(
                 [few_stage[2 * k, :, cols], few_stage[2 * k + 1, :, cols]], 1
             )
-    for d in range(1, n):
-        exchange(3, d, pack.at[lax.rem(w + d, n)], p_all.at[w])
+
+    def exchange_rest(target):
+        remote(
+            pack.at[target], p_all.at[w], a_send.at[3], a_recv.at[3], {"wide": target, "heads": h}
+        ).start()
+
+    exchange_rest(mate)
+
+    @pl.when(jnp.logical_not(inner))
+    def _():
+        exchange_rest(far_end)
+
     own_pack = pltpu.make_async_copy(pack.at[w], p_all.at[w], local.at[0])
     own_pack.start()
     own.pop().wait()
@@ -351,15 +379,8 @@
                 (few, rows), drop
             )
 
-    mine = h * n + w
-    side = w // (n // 2)
-    mate = w + 1 - 2 * lax.rem(w, 2)
-    across_side = n // 2 - side
-    far_start = (1 - side) * (n // 2)
-    inner = (w > 0) & (w < n - 1)
     splits = (part_few * n + half // 2, half // 2)
     starts = (0, splits[0])
-    x_copies = {}
 
     def chunk(ref, kind):
         if kind == 0:
@@ -369,61 +390,60 @@
     def buffers(kind):
         return (o_self, r_self) if kind == 0 else (o_rest, r_rest)
 
-    def across(kind, d):
+    def spread(kind, d):
         source, landing = buffers(kind)
-        copy = remote(
-            source.at[lax.rem(h + d, n)], landing.at[mine],
-            x_send.at[kind, d], x_recv.at[kind, d], place(0, d),
-        )
-        copy.start()
-        x_copies[kind, d] = copy
-
-    def along(kind, d):
-        source, landing = buffers(kind)
-        slot = lax.rem(h + n - d, n) * n + w
-        piece = chunk(source.at[h] if d == 0 else landing.at[slot], kind)
-        where = chunk(landing.at[slot], kind)
-        for k, device, role in ((0, mate, 0), (1, across_side, 1 + lax.rem(w, 2))):
-            copy = remote(
-                piece, where, z_send.at[kind, d, k], z_recv.at[kind, d, role],
-                {"wide": device, "heads": h},
-            )
-            copy.start()
-            sent.append(copy)
-
-    def arrival(kind, d, k):
+        part = lax.rem(h + d, n)
+        piece, where = chunk(source.at[part], kind), chunk(landing.at[mine], kind)
+        if d:
+            remote(
+                piece, where, x_send.at[kind], x_recv.at[kind], {"wide": w, "heads": part}
+            ).start()
+        remote(
+            piece, where, z_send.at[kind], z_recv.at[kind, d, lax.rem(w, 2)],
+            {"wide": across_side, "heads": part},
+        ).start()
+        remote(
+            piece, where, z_send.at[kind], m_recv.at[kind], {"wide": mate, "heads": part}
+        ).start()
+
+    def far_piece(kind, d, k):
+        slot = lax.rem(h + n - d, n) * n + far_start + k
+        return chunk(buffers(kind)[1].at[slot], kind)
+
+    def forward(kind, d, ks):
+        for k in ks:
+            piece = far_piece(kind, d, k)
+            settle(piece, z_recv.at[kind, d, k])
+            remote(
+                piece, piece, r_send.at[kind], z_recv.at[kind, d, k],
+                {"wide": mate, "heads": h},
+            ).start()
+
+    def many(kind, count):
         landing = buffers(kind)[1]
-        slot = lax.rem(h + n - d, n) * n + far_start + k
-        where = chunk(landing.at[slot], kind)
-        return remote(
-            where, where, r_send.at[kind, d, k], z_recv.at[kind, d, 1 + k],
-            {"wide": mate, "heads": h},
-        )
-
-    def forward(kind, d):
-        for k in range(2):
-            copy = arrival(kind, d, k)
-            copy.wait_recv()
-
-            @pl.when(inner)
-            def _():
-                copy.start()
-
-    def from_mate(kind, d):
-        landing = buffers(kind)[1]
-        slot = lax.rem(h + n - d, n) * n + mate
-        where = chunk(landing.at[slot], kind)
-        remote(
-            where, where, z_send.at[kind, d, 0], z_recv.at[kind, d, 0],
-            {"wide": mate, "heads": h},
-        ).wait_recv()
+        if kind == 0:
+            return landing.at[:count]
+        return landing.at[:count, pl.ds(starts[kind - 1], splits[kind - 1])]
+
+    def gathered(kind):
+        settle(many(kind, n - 1), x_recv.at[kind])
+        settle(many(kind, n), m_recv.at[kind])
+
+        @pl.when(jnp.logical_not(inner))
+        def _():
+            for d in range(n):
+                for k in range(2):
+                    settle(far_piece(kind, d, k), z_recv.at[kind, d, k])
 
     with scope("T1self"):
-        for copy in own[:3]:
-            copy.wait()
-        for i in range(3):
-            for d in range(1, n):
-                a_copies[i, d].wait_recv()
+        for i, target in enumerate((q_all, k_all, v_all)):
+            own[i].wait()
+            settle(target.at[: n - 1], a_recv.at[i])
+
+    @pl.when(inner)
+    def _():
+        exchange_rest(far_end)
+
     keys = k_all[...].reshape(n * rows, HDV)
     values = v_all[...].reshape(n * rows, HDV)
 
@@ -431,30 +451,30 @@
         at = pl.multiple_of(lax.rem(h + d, n) * part_rows, part_rows)
         return scored(q_all[:, pl.ds(at, part_rows), :].reshape(rows, HDV), keys)
 
-    scores = self_scores(0)
-    for d in range(n):
-        following = self_scores(d + 1) if d + 1 < n else None
+    turns = list(range(1, n)) + [0]
+    scores = self_scores(turns[0])
+    for turn, d in enumerate(turns):
+        following = self_scores(turns[turn + 1]) if turn + 1 < n else None
         weights, sums = softmax(scores, HDV)
         result = (mixed(weights, values) / sums).astype(bf16)
         scores = following
         o_self[pl.ds(lax.rem(h + d, n), 1)] = result[None]
-        if d:
-            across(0, d)
-        else:
+        if not d:
             r_self[pl.ds(mine, 1)] = result[None]
-            along(0, 0)
-        if d > 1:
-            x_copies[0, d - 1].wait_recv()
-            along(0, d - 1)
-    send_weights(1)
-    with scope("T2x"):
-        x_copies[0, n - 1].wait_recv()
-    along(0, n - 1)
-
+        spread(0, d)
+    exchange_rest(across_side)
+    with scope("T2weights"):
+        swap_weights(0)
+        swap_weights(1)
+    send_weights(2)
+    with scope("T2forward"):
+        @pl.when(inner)
+        def _():
+            for d in turns:
+                forward(0, d, range(2))
     with scope("T3rest"):
         own_pack.wait()
-        for d in range(1, n):
-            a_copies[3, d].wait_recv()
+        settle(p_all.at[: n - 1], a_recv.at[3])
     at = rows + half
     lane = lax.broadcasted_iota(jnp.int32, (n * few, 2 * HDA), 1)
     left = lane < HDA
@@ -482,117 +502,73 @@
         o_rest[t, : n * part_few, :] = jnp.concatenate(
             [audio[j * few + t * part_few : j * few + (t + 1) * part_few, :] for j in range(n)], 0
         )
-    forward(0, 0)
-
     def cross_scores(d):
         begin = pl.multiple_of(lax.rem(h + d, n) * part_rows, part_rows)
         queries = p_all[:, pl.ds(begin, part_rows), :].reshape(rows, 2 * HDA)
         return scored(queries, key_left) + tall_bias[...]
 
     low = lax.broadcasted_iota(jnp.int32, (half, 2 * HDA), 1) < HDA
-    scores = cross_scores(0)
-    for d in range(n):
-        following = cross_scores(d + 1) if d + 1 < n else None
+    scores = cross_scores(turns[0])
+    for turn, d in enumerate(turns):
+        following = cross_scores(turns[turn + 1]) if turn + 1 < n else None
         weights, sums = softmax(scores, HDA)
         result = mixed(weights, twice) / sums
         scores = following
         block = lax.rem(h + d, n)
-        packed = jnp.where(low, result[:half], result[half:]).astype(bf16)
+        upper = [result[j * part_rows : (j + 1) * part_rows] for j in reversed(range(n // 2))]
+        packed = jnp.where(low, jnp.concatenate(upper, 0), result[half:]).astype(bf16)
         o_rest[pl.ds(block, 1), n * part_few :, :] = packed[None]
-        if d:
-            across(1, d)
-            forward(0, d)
-        else:
+        if not d:
             r_rest[pl.ds(mine, 1)] = o_rest[pl.ds(h, 1)]
-            along(1, 0)
-            along(2, 0)
-        if d > 1:
-            x_copies[1, d - 1].wait_recv()
-            along(1, d - 1)
-            along(2, d - 1)
-    send_weights(2)
-    with scope("T4x"):
-        x_copies[1, n - 1].wait_recv()
-    along(1, n - 1)
-    along(2, n - 1)
-
+        spread(1, d)
+        spread(2, d)
+    with scope("T4weights"):
+        swap_weights(2)
+        pass_weights(0)
+        pass_weights(1)
+    with scope("T4forward"):
+        @pl.when(inner)
+        def _():
+            for which in range(2):
+                for kind in (1, 2):
+                    for d in turns:
+                        forward(kind, d, [lax.rem(w + which, 2)])
     with scope("T5w"):
         own[3].wait()
         own[4].wait()
-        pass_weights(0)
         settle_weights(0)
     with scope("T6self"):
-        for d in range(n):
-            from_mate(0, d)
+        gathered(0)
     heads = n * n
     joined = jnp.concatenate([r_self[s] for s in range(heads)], 1)
     totals[...] = jnp.dot(
         joined, ws_all[...].reshape(-1, ws.shape[1]), preferred_element_type=jnp.float32
     )
     with scope("T7w"):
-        pass_weights(1)
         settle_weights(1)
-        pass_weights(2)
-        settle_weights(2)
-
-    chunks = d_send.shape[0] - 1
-    width = ws.shape[1] // chunks
-    d_copies, last = {}, []
-
-    def cut(ref, c):
-        return ref if c == 0 else ref.at[:, (c - 1) * width : c * width]
-
-    def rows_of(ref, c, block):
-        size = part_few if c == 0 else part_rows
-        return cut(ref.at[pl.ds(pl.multiple_of(block * size, size), size)], c)
-
-    def first_hop(c, b):
-        source, middle = (sum_a, mid_a) if c == 0 else (sum_v, mid_v)
-
-        @pl.when(w != b)
+
+    def rows_of(ref, block, size):
+        return ref.at[pl.ds(pl.multiple_of(block * size, size), size)]
+
+    def deliver(c, b):
+        source, out, size = ((sum_v, out_v, part_rows), (sum_a, out_a, part_few))[c]
+        piece, target = rows_of(source, b, size), rows_of(out, h, size)
+        away = (w != b) | (w != h)
+
+        @pl.when(away)
         def _():
             remote(
-                rows_of(source, c, b), cut(middle.at[w], c),
-                d_send.at[c, b], d_recv.at[c, w], {"wide": b, "heads": h},
+                piece, target, e_send.at[c], e_recv.at[c], {"wide": b, "heads": w}
             ).start()
 
-    def second_hop(c, origin):
-        source, middle, out = (sum_a, mid_a, out_a) if c == 0 else (sum_v, mid_v, out_v)
-
-        def go(ready):
-            target = rows_of(out, c, h)
-
-            @pl.when(origin != h)
-            def _():
-                remote(
-                    ready, target, e_send.at[c, origin], e_recv.at[c, h],
-                    {"wide": w, "heads": origin},
-                ).start()
-
-            @pl.when(origin == h)
-            def _():
-                pltpu.make_async_copy(ready, target, e_send.at[c, origin]).start()
-
-        @pl.when(w == origin)
+        @pl.when(jnp.logical_not(away))
         def _():
-            go(rows_of(source, c, w))
-
-        @pl.when(w != origin)
-        def _():
-            piece = cut(middle.at[origin], c)
-            remote(
-                piece, piece, d_send.at[c, origin], d_recv.at[c, origin],
-                {"wide": origin, "heads": h},
-            ).wait_recv()
-            go(piece)
+            pltpu.make_async_copy(piece, target, e_recv.at[c]).start()
 
     flat_c = wc_all[...].reshape(-1, wc.shape[1])
     for u in range(2):
         with scope("T8gather%d" % u):
-            for d in range(n):
-                forward(1 + u, d)
-            for d in range(n):
-                from_mate(1 + u, d)
+            gathered(1 + u)
         begin = n * part_few + u * (half // 2)
         piece = slice(begin, begin + half // 2)
         crossed = jnp.concatenate(
@@ -605,73 +581,61 @@
         products = jnp.dot(crossed, flat_c, preferred_element_type=jnp.float32)
         size = half // 2
         for k in range(2):
-            where = slice((u + 2 * k) * size, (u + 2 * k + 1) * size)
+            b = (n // 2 - 1 - u, n // 2 + u)[k]
+            where = slice(b * size, (b + 1) * size)
             sum_v[where, :] = (
                 totals[where, :] + products[k * size : (k + 1) * size, :]
             ).astype(bf16)
-        for c in range(1, chunks + 1):
-            for k in (1 - u, u):
-                first_hop(c, u + 2 * k)
+        if u == 1:
+            with scope("T8sent"):
+                @pl.when(inner)
+                def _():
+                    for kind in range(3):
+                        settle(many(kind, 2 * n), r_send.at[kind])
+
+        for b in (n // 2 - 1 - u, n // 2 + u):
+            deliver(0, b)
         if u == 0:
+            with scope("T8weights"):
+                pass_weights(2)
+                settle_weights(2)
             audio_joined = jnp.concatenate([r_rest[s, : n * part_few, :] for s in range(heads)], 1)
             sum_a[...] = jnp.dot(
                 audio_joined, wa_all[...].reshape(-1, aso.shape[1]),
                 preferred_element_type=jnp.float32,
             ).astype(bf16)
             for b in range(n):
-                first_hop(0, b)
-    order = list(range(1, chunks + 1)) + [0]
+                deliver(1, b)
+
     with scope("T9results"):
-        for c in order:
-            for origin in range(n):
-                second_hop(c, origin)
-
-    with scope("TAout"):
-        for c in order:
-            out = out_a if c == 0 else out_v
-            for who in range(n):
-                @pl.when(who != h)
-                def _():
-                    target = rows_of(out, c, who)
-                    remote(
-                        target, target, e_send.at[c, who], e_recv.at[c, who],
-                        {"wide": w, "heads": who},
-                    ).wait()
-
-                @pl.when(who == h)
-                def _():
-                    target = rows_of(out, c, h)
-                    pltpu.make_async_copy(target, target, e_send.at[c, who]).wait()
+        settle(out_v, e_recv.at[0])
+        settle(out_a, e_recv.at[1])
 
     with scope("TBsends"):
-        for copy in (
-            list(a_copies.values()) + list(w_copies.values()) + sum(f_copies.values(), [])
-            + list(x_copies.values()) + sent
-        ):
-            copy.wait_send()
-        for c in order:
-            source = sum_a if c == 0 else sum_v
-            for b in range(n):
-                @pl.when(w != b)
-                def _():
-                    piece = rows_of(source, c, b)
-                    remote(
-                        piece, piece, d_send.at[c, b], d_recv.at[c, b], {"wide": b, "heads": h}
-                    ).wait_send()
-
-        @pl.when(inner)
-        def _():
-            for kind in range(3):
-                for d in range(n):
-                    for k in range(2):
-                        arrival(kind, d, k).wait_send()
+        for i, target in enumerate((q_all, k_all, v_all, p_all)):
+            settle(target.at[: n - 1], a_send.at[i])
+        for i in range(3):
+            settle(part_of(targets[i].at[h], g), w_send.at[i, 0])
+            settle(targets[i].at[h], w_send.at[i, 1])
+            settle(part_of(targets[i].at[h], g), w_send.at[i, 2])
+            settle(targets[i].at[h], w_send.at[i, 3])
+        for kind in range(3):
+            settle(many(kind, n - 1), x_send.at[kind])
+            settle(many(kind, 2 * n), z_send.at[kind])
+        for c, (ref, size) in enumerate(((sum_v, part_rows), (sum_a, part_few))):
+            settle(ref.at[: (n - 1) * size], e_send.at[c])
+
+            @pl.when(w != h)
+            def _():
+                settle(ref.at[:size], e_send.at[c])
 
 
 def shards(*args):
     n = lax.axis_size("wide")
     count = lax.axis_size("heads")
     head_count = args[2].shape[1] // HDV
-    if not (n == count == head_count == 2 * REACH and args[5].shape[0] % (16 * n) == 0):
+    paired = lax.axis_size("groups") == 2
+    if not (paired and n == count == head_count == 2 * REACH and args[5].shape[0] % (16 * n) == 0):
         return general_shards(*args)
     (video_hidden, audio_hidden, vq, vk, vv, aq, ak, av, cvq, cak, cav, caq, cvk, cvv,
      vso, vco, aso, aco, table) = args
@@ -679,7 +643,6 @@
     depth = rows + rows // 2 + 3 * few
     anywhere = pl.BlockSpec(memory_space=pl.ANY)
     bf16, f32 = jnp.bfloat16, jnp.float32
-    chunks = max(1, vso.shape[1] // 512)
     rest = rows // 2 + few
     dma = pltpu.SemaphoreType.DMA
     video_sum, audio_sum = pl.pallas_call(
@@ -710,15 +673,11 @@
             pltpu.VMEM(video_hidden.shape, f32),
             pltpu.VMEM(video_hidden.shape, bf16),
             pltpu.VMEM(audio_hidden.shape, bf16),
-            pltpu.VMEM((n, rows // n, video_hidden.shape[1]), bf16),
-            pltpu.VMEM((n, few // n, audio_hidden.shape[1]), bf16),
-            dma((4, n)), dma((4, n)),
-            dma((3, n)), dma((3, n)),
-            dma((3, n)), dma((3, n)),
-            dma((2, n)), dma((2, n)),
-            dma((3, n, 2)), dma((3, n, 3)), dma((3, n, 2)),
-            dma((1 + chunks, n)), dma((1 + chunks, n)),
-            dma((1 + chunks, n)), dma((1 + chunks, n)),
+            dma((4,)), dma((4,)),
+            dma((3, 4)), dma((3, 4)),
+            dma((3,)), dma((3,)),
+            dma((3,)), dma((3, n, 2)), dma((3,)), dma((3,)),
+            dma((2,)), dma((2,)),
             dma((15,)),
         ],
         compiler_params=pltpu.CompilerParams(collective_id=0, has_side_effects=True),

time: 100 us -> 82.8 us (0.83)
  the two profiles are of different devices: /device:TPU:29 before, /device:TPU:1 now
where the time goes in v2:
time: 82.8 us; the launch traced here: 82.2 us
  Pallas kernels  78.8 us (95%)
  other arithmetic  2.71 us (3%)
    pallas_call x1, Pallas kernels, shards(): pl.pallas_call(functools.partial(joint_kernel, n), out_shape=(jax.ShapeDt...  78.8 us
    convert_element_type x2, other arithmetic, shards(): return (video_out.astype(bf16), audio_out.astype(bf16))  2.71 us

profile of v2, /device:TPU:1, one launch (start us, length us, event | category | flops | bytes accessed | tf_op | source)
XLA Modules:
  0.0 82.2 jit_solution(14069740844753888196)
XLA Ops:
  0.6 0.0 copy-start
  0.6 78.8 %joint.1 = (bf16[256,1024]{1,0:T(8,128)(2,1)}, bf16[64,512]{1,0:T(8,128)(2,1)}) custom-call(bf16[256,512]{1,0:T(8,128)(2,1)} %vq.1, bf16[256,512]{1,0:T(8,128)(2,1)} %vk.1, bf16[256,512]{1,0:T(8,128)(2,1)} %vv.1, bf16[256,256]{1,0:T(8,128)(2,1)} %cvq.1, bf16[256,256]{1,0:T(8,128)(2,1)} %cvk.1, bf16[256,256]{1,0:T(8,128)(2,1)} %cvv.1, bf16[64,256]{1,0:T(8,128)(2,1)} %aq.1, ...), custom_call_target="tpu_custom_call" | custom-call | tf_op jit(solution)/shard_map/joint/pallas_call | solution.py:648
  79.4 0.0 copy-done
  79.5 0.0 copy-start.1
  79.5 0.0 copy-start.2
  79.5 2.1 %add_convert_fusion = bf16[256,1024]{1,0:T(8,128)(2,1)} fusion(bf16[256,1024]{1,0:T(8,128)(2,1)} %get-tuple-element.4, bf16[256,1024]{1,0:T(8,128)(2,1)S(1)} %copy-done), kind=kLoop, calls=%fused_computation | loop fusion | flops 1048576 | bytes 1572864 | tf_op jit(solution)/shard_map/convert_element_type | solution.py:688
  81.5 0.0 copy-done.1
  81.5 0.0 copy-done.2
  81.5 0.6 add_convert_fusion.1
Async XLA Ops:
  0.6 78.8 %copy-start = (bf16[256,1024]{1,0:T(8,128)(2,1)S(1)}, bf16[256,1024]{1,0:T(8,128)(2,1)}, u32[]{:S(2)}) copy-start(bf16[256,1024]{1,0:T(8,128)(2,1)} %param.19) | copy-start | bytes 1572868
  79.5 2.1 %copy-start.1 = (bf16[64,512]{1,0:T(8,128)(2,1)S(1)}, bf16[64,512]{1,0:T(8,128)(2,1)}, u32[]{:S(2)}) copy-start(bf16[64,512]{1,0:T(8,128)(2,1)} %param.20) | copy-start | bytes 196612
  79.5 2.1 %copy-start.2 = (bf16[64,512]{1,0:T(8,128)(2,1)S(1)}, bf16[64,512]{1,0:T(8,128)(2,1)}, u32[]{:S(2)}) copy-start(bf16[64,512]{1,0:T(8,128)(2,1)} %get-tuple-element.5) | copy-start | bytes 196612

commit v3 on v2

--- a/solution.py
+++ b/solution.py
@@ -208,7 +208,7 @@
     n,
     vq, vk, vv, cvq, cvk, cvv, aq, ak, av, caq, cak, cav, ws, wc, aso, aco, table,
     out_v, out_a,
-    q_all, k_all, v_all, wide_stage, few_stage, pack, p_all, ws_all, wc_all, wa_all,
+    q_all, k_all, v_all, self_stage, wide_stage, few_stage, pack, p_all, ws_all, wc_all, wa_all,
     tall_bias, wide_bias, o_self, o_rest, r_self, r_rest, totals, sum_v, sum_a,
     a_send, a_recv, w_send, w_recv, x_send, x_recv, z_send, z_recv, m_recv, r_send,
     e_send, e_recv, local,
@@ -256,6 +256,13 @@
             copy.start()
         return copies
 
+    streams = ((vq, q_all), (vk, k_all), (vv, v_all))
+    self_staged = start(
+        [
+            pltpu.make_async_copy(source, self_stage.at[i], local.at[15 + i])
+            for i, (source, _) in enumerate(streams)
+        ]
+    )
     staged = start(
         [
             pltpu.make_async_copy(source, wide_stage.at[i], local.at[i])
@@ -269,7 +276,7 @@
     own = start(
         [
             pltpu.make_async_copy(head_cols(source, w), target.at[w], local.at[9 + i])
-            for i, (source, target) in enumerate(((vq, q_all), (vk, k_all), (vv, v_all)))
+            for i, (source, target) in enumerate(streams)
         ]
         + [
             pltpu.make_async_copy(source, target.at[h], local.at[12 + i])
@@ -283,15 +290,17 @@
                 source.at[j * HDA : (j + 1) * HDA], wa_all.at[h, at : at + HDA], local.at[14]
             ).start()
     own.append(pltpu.make_async_copy(wa_all.at[h], wa_all.at[h], local.at[14]))
+    for copy in self_staged:
+        copy.wait()
     with scope("T0barrier"):
         pl.semaphore_wait(barrier, len(others) + 1)
 
     far_end = (1 - side) * (n - 1)
 
     def exchange(target):
-        for i, (source, landing) in enumerate(((vq, q_all), (vk, k_all), (vv, v_all))):
+        for i, (_, landing) in enumerate(streams):
             remote(
-                head_cols(source, target), landing.at[w], a_send.at[i], a_recv.at[i],
+                head_cols(self_stage.at[i], target), landing.at[w], a_send.at[i], a_recv.at[i],
                 {"wide": target, "heads": h},
             ).start()
 
@@ -355,15 +364,18 @@
             pack.at[target], p_all.at[w], a_send.at[3], a_recv.at[3], {"wide": target, "heads": h}
         ).start()
 
+    outer = jnp.logical_not(inner)
     exchange_rest(mate)
 
-    @pl.when(jnp.logical_not(inner))
+    @pl.when(outer)
     def _():
         exchange_rest(far_end)
+
 
     own_pack = pltpu.make_async_copy(pack.at[w], p_all.at[w], local.at[0])
     own_pack.start()
     own.pop().wait()
+    send_weights(2)
     share_weights(2)
 
     for i in range(n):
@@ -390,28 +402,48 @@
     def buffers(kind):
         return (o_self, r_self) if kind == 0 else (o_rest, r_rest)
 
-    def spread(kind, d):
+    orders = ((1, 0, 2, 3), (2, 3, 1, 0))
+
+    def moved(e):
+        return lax.rem(h // 2 + e // 2, 2) * 2 + lax.rem(h + e, 2)
+
+    def turn_of(i):
+        return orders[0][i] + lax.rem(w, 2) * (orders[1][i] - orders[0][i])
+
+    def outgoing(kind, i):
         source, landing = buffers(kind)
-        part = lax.rem(h + d, n)
-        piece, where = chunk(source.at[part], kind), chunk(landing.at[mine], kind)
-        if d:
+        d = turn_of(i)
+        part = moved(d)
+        return d, part, chunk(source.at[part], kind), chunk(landing.at[mine], kind)
+
+    def to_plane(kind, i):
+        _, part, piece, where = outgoing(kind, i)
+
+        @pl.when(part != h)
+        def _():
             remote(
                 piece, where, x_send.at[kind], x_recv.at[kind], {"wide": w, "heads": part}
             ).start()
+
+    def to_across(kind, i):
+        d, part, piece, where = outgoing(kind, i)
         remote(
             piece, where, z_send.at[kind], z_recv.at[kind, d, lax.rem(w, 2)],
             {"wide": across_side, "heads": part},
         ).start()
+
+    def to_mate(kind, i):
+        _, part, piece, where = outgoing(kind, i)
         remote(
             piece, where, z_send.at[kind], m_recv.at[kind], {"wide": mate, "heads": part}
         ).start()
 
     def far_piece(kind, d, k):
-        slot = lax.rem(h + n - d, n) * n + far_start + k
-        return chunk(buffers(kind)[1].at[slot], kind)
-
-    def forward(kind, d, ks):
+        return chunk(buffers(kind)[1].at[moved(d) * n + far_start + k], kind)
+
+    def forward(kind, i, ks):
         for k in ks:
+            d = orders[0][i] + k * (orders[1][i] - orders[0][i])
             piece = far_piece(kind, d, k)
             settle(piece, z_recv.at[kind, d, k])
             remote(
@@ -429,7 +461,7 @@
         settle(many(kind, n - 1), x_recv.at[kind])
         settle(many(kind, n), m_recv.at[kind])
 
-        @pl.when(jnp.logical_not(inner))
+        @pl.when(outer)
         def _():
             for d in range(n):
                 for k in range(2):
@@ -447,34 +479,41 @@
     keys = k_all[...].reshape(n * rows, HDV)
     values = v_all[...].reshape(n * rows, HDV)
 
-    def self_scores(d):
-        at = pl.multiple_of(lax.rem(h + d, n) * part_rows, part_rows)
+    def self_scores(i):
+        at = pl.multiple_of(moved(turn_of(i)) * part_rows, part_rows)
         return scored(q_all[:, pl.ds(at, part_rows), :].reshape(rows, HDV), keys)
 
-    turns = list(range(1, n)) + [0]
-    scores = self_scores(turns[0])
-    for turn, d in enumerate(turns):
-        following = self_scores(turns[turn + 1]) if turn + 1 < n else None
+    scores = self_scores(0)
+    for i in range(n):
+        following = self_scores(i + 1) if i + 1 < n else None
         weights, sums = softmax(scores, HDV)
         result = (mixed(weights, values) / sums).astype(bf16)
         scores = following
-        o_self[pl.ds(lax.rem(h + d, n), 1)] = result[None]
-        if not d:
-            r_self[pl.ds(mine, 1)] = result[None]
-        spread(0, d)
-    exchange_rest(across_side)
+        o_self[pl.ds(moved(turn_of(i)), 1)] = result[None]
+        to_plane(0, i)
+        to_across(0, i)
+        to_mate(0, i)
+    r_self[pl.ds(mine, 1)] = o_self[pl.ds(h, 1)]
+
+    @pl.when(inner)
+    def _():
+        exchange_rest(across_side)
+
     with scope("T2weights"):
         swap_weights(0)
         swap_weights(1)
-    send_weights(2)
     with scope("T2forward"):
         @pl.when(inner)
         def _():
-            for d in turns:
-                forward(0, d, range(2))
+            for k in (lax.rem(w, 2), lax.rem(w + 1, 2)):
+                for i in range(n):
+                    forward(0, i, [k])
+
+    swap_weights(2)
     with scope("T3rest"):
         own_pack.wait()
         settle(p_all.at[: n - 1], a_recv.at[3])
+
     at = rows + half
     lane = lax.broadcasted_iota(jnp.int32, (n * few, 2 * HDA), 1)
     left = lane < HDA
@@ -502,37 +541,65 @@
         o_rest[t, : n * part_few, :] = jnp.concatenate(
             [audio[j * few + t * part_few : j * few + (t + 1) * part_few, :] for j in range(n)], 0
         )
-    def cross_scores(d):
-        begin = pl.multiple_of(lax.rem(h + d, n) * part_rows, part_rows)
+    def cross_scores(i):
+        begin = pl.multiple_of(moved(turn_of(i)) * part_rows, part_rows)
         queries = p_all[:, pl.ds(begin, part_rows), :].reshape(rows, 2 * HDA)
         return scored(queries, key_left) + tall_bias[...]
 
     low = lax.broadcasted_iota(jnp.int32, (half, 2 * HDA), 1) < HDA
-    scores = cross_scores(turns[0])
-    for turn, d in enumerate(turns):
-        following = cross_scores(turns[turn + 1]) if turn + 1 < n else None
+    scores = cross_scores(0)
+    for i in range(n):
+        following = cross_scores(i + 1) if i + 1 < n else None
         weights, sums = softmax(scores, HDA)
         result = mixed(weights, twice) / sums
         scores = following
-        block = lax.rem(h + d, n)
+        block = moved(turn_of(i))
         upper = [result[j * part_rows : (j + 1) * part_rows] for j in reversed(range(n // 2))]
         packed = jnp.where(low, jnp.concatenate(upper, 0), result[half:]).astype(bf16)
         o_rest[pl.ds(block, 1), n * part_few :, :] = packed[None]
-        if not d:
-            r_rest[pl.ds(mine, 1)] = o_rest[pl.ds(h, 1)]
-        spread(1, d)
-        spread(2, d)
+        to_plane(1, i)
+
+        @pl.when(inner)
+        def _():
+            to_across(1, i)
+            to_mate(1, i)
+
+    r_rest[pl.ds(mine, 1)] = o_rest[pl.ds(h, 1)]
     with scope("T4weights"):
-        swap_weights(2)
-        pass_weights(0)
-        pass_weights(1)
+        @pl.when(inner)
+        def _():
+            for i in range(3):
+                pass_weights(i)
+
+    ends, peers = [lax.rem(w, 2)], [lax.rem(w + 1, 2)]
     with scope("T4forward"):
+        for i in range(n):
+            to_plane(2, i)
+
+        @pl.when(outer)
+        def _():
+            for kind in (1, 2):
+                for i in range(n):
+                    to_mate(kind, i)
+            exchange_rest(across_side)
+
         @pl.when(inner)
         def _():
-            for which in range(2):
-                for kind in (1, 2):
-                    for d in turns:
-                        forward(kind, d, [lax.rem(w + which, 2)])
+            for i in range(n):
+                forward(1, i, ends)
+            for i in range(n):
+                to_across(2, i)
+                to_mate(2, i)
+            for kind, ks in ((1, peers), (2, ends), (2, peers)):
+                for i in range(n):
+                    forward(kind, i, ks)
+
+    with scope("T5pass"):
+        @pl.when(outer)
+        def _():
+            for i in range(3):
+                pass_weights(i)
+
     with scope("T5w"):
         own[3].wait()
         own[4].wait()
@@ -544,6 +611,13 @@
     totals[...] = jnp.dot(
         joined, ws_all[...].reshape(-1, ws.shape[1]), preferred_element_type=jnp.float32
     )
+
+    @pl.when(outer)
+    def _():
+        for kind in (1, 2):
+            for i in range(n):
+                to_across(kind, i)
+
     with scope("T7w"):
         settle_weights(1)
 
@@ -597,7 +671,6 @@
             deliver(0, b)
         if u == 0:
             with scope("T8weights"):
-                pass_weights(2)
                 settle_weights(2)
             audio_joined = jnp.concatenate([r_rest[s, : n * part_few, :] for s in range(heads)], 1)
             sum_a[...] = jnp.dot(
@@ -651,12 +724,13 @@
             jax.ShapeDtypeStruct(video_hidden.shape, bf16),
             jax.ShapeDtypeStruct(audio_hidden.shape, bf16),
         ),
-        in_specs=[anywhere] * 16 + [pl.BlockSpec(memory_space=pltpu.SMEM)],
+        in_specs=[pl.BlockSpec(memory_space=pltpu.HBM)] * 16 + [pl.BlockSpec(memory_space=pltpu.SMEM)],
         out_specs=(anywhere, anywhere),
         scratch_shapes=[
             pltpu.VMEM((n, rows, HDV), bf16),
             pltpu.VMEM((n, rows, HDV), bf16),
             pltpu.VMEM((n, rows, HDV), bf16),
+            pltpu.VMEM((3,) + vq.shape, bf16),
             pltpu.VMEM((3,) + cvq.shape, bf16),
             pltpu.VMEM((6,) + aq.shape, bf16),
             pltpu.VMEM((n, depth, 2 * HDA), bf16),
@@ -678,11 +752,20 @@
             dma((3,)), dma((3,)),
             dma((3,)), dma((3, n, 2)), dma((3,)), dma((3,)),
             dma((2,)), dma((2,)),
-            dma((15,)),
+            dma((18,)),
         ],
-        compiler_params=pltpu.CompilerParams(collective_id=0, has_side_effects=True),
+        compiler_params=pltpu.CompilerParams(
+            collective_id=0, has_side_effects=True, vmem_limit_bytes=48 * 1024 * 1024
+        ),
         name="joint",
-    )(vq, vk, vv, cvq, cvk, cvv, aq, ak, av, caq, cak, cav, vso, vco, aso, aco, table)
+    )(
+        *(
+            pltpu.with_memory_space_constraint(operand, pltpu.HBM)
+            for operand in (
+                vq, vk, vv, cvq, cvk, cvv, aq, ak, av, caq, cak, cav, vso, vco, aso, aco, table
+            )
+        )
+    )
     video_out = video_hidden.astype(f32) + video_sum.astype(f32)
     audio_out = audio_hidden.astype(f32) + audio_sum.astype(f32)
     return (video_out.astype(bf16), audio_out.astype(bf16))

time: 82.8 us -> 78.2 us (0.944)
  the two profiles are of different devices: /device:TPU:1 before, /device:TPU:2 now
where the time goes in v3:
time: 78.2 us; the launch traced here: 78 us
  Pallas kernels  75.7 us (97%)
  other arithmetic  1.64 us (2%)
    pallas_call x1, Pallas kernels, shards(): pl.pallas_call(functools.partial(joint_kernel, n), out_shape=(jax.ShapeDt...  75.7 us
    convert_element_type x2, other arithmetic, shards(): return (video_out.astype(bf16), audio_out.astype(bf16))  1.64 us

profile of v3, /device:TPU:2, one launch (start us, length us, event | category | flops | bytes accessed | tf_op | source)
XLA Modules:
  0.0 78.0 jit_solution(15123998397351212090)
XLA Ops:
  0.6 0.0 copy-start
  0.6 75.7 %joint.1 = (bf16[256,1024]{1,0:T(8,128)(2,1)S(1)}, bf16[64,512]{1,0:T(8,128)(2,1)S(1)}) custom-call(bf16[256,512]{1,0:T(8,128)(2,1)} %vq.1, bf16[256,512]{1,0:T(8,128)(2,1)} %vk.1, bf16[256,512]{1,0:T(8,128)(2,1)} %vv.1, bf16[256,256]{1,0:T(8,128)(2,1)} %cvq.1, bf16[256,256]{1,0:T(8,128)(2,1)} %cvk.1, bf16[256,256]{1,0:T(8,128)(2,1)} %cvv.1, ...), custom_call_target="tpu_custom_call" | custom-call | tf_op jit(solution)/shard_map/joint/pallas_call | solution.py:721
  76.4 0.0 copy-done
  76.4 0.0 copy-start.1
  76.4 1.0 %add_convert_fusion = bf16[256,1024]{1,0:T(8,128)(2,1)} fusion(bf16[256,1024]{1,0:T(8,128)(2,1)S(1)} %get-tuple-element.4, bf16[256,1024]{1,0:T(8,128)(2,1)S(1)} %copy-done), kind=kLoop, calls=%fused_computation | loop fusion | flops 1048576 | bytes 1572864 | tf_op jit(solution)/shard_map/convert_element_type | solution.py:771
  77.4 0.0 copy-done.1
  77.4 0.6 add_convert_fusion.1
Async XLA Ops:
  0.6 75.7 %copy-start = (bf16[256,1024]{1,0:T(8,128)(2,1)S(1)}, bf16[256,1024]{1,0:T(8,128)(2,1)}, u32[]{:S(2)}) copy-start(bf16[256,1024]{1,0:T(8,128)(2,1)} %param.19) | copy-start | bytes 1572868
  76.4 1.0 %copy-start.1 = (bf16[64,512]{1,0:T(8,128)(2,1)S(1)}, bf16[64,512]{1,0:T(8,128)(2,1)}, u32[]{:S(2)}) copy-start(bf16[64,512]{1,0:T(8,128)(2,1)} %param.20) | copy-start | bytes 196612

commit v4 on v3

--- a/solution.py
+++ b/solution.py
@@ -459,7 +459,13 @@
 
     def gathered(kind):
         settle(many(kind, n - 1), x_recv.at[kind])
-        settle(many(kind, n), m_recv.at[kind])
+        if kind != 1:
+            settle(many(kind, n), m_recv.at[kind])
+        else:
+            @pl.when(inner)
+            def _():
+                settle(many(kind, n), m_recv.at[kind])
+
 
         @pl.when(outer)
         def _():
@@ -508,6 +514,9 @@
             for k in (lax.rem(w, 2), lax.rem(w + 1, 2)):
                 for i in range(n):
                     forward(0, i, [k])
+            with scope("T2pass"):
+                pass_weights(0)
+                pass_weights(1)
 
     swap_weights(2)
     with scope("T3rest"):
@@ -546,6 +555,7 @@
         queries = p_all[:, pl.ds(begin, part_rows), :].reshape(rows, 2 * HDA)
         return scored(queries, key_left) + tall_bias[...]
 
+    ends, peers = [lax.rem(w, 2)], [lax.rem(w + 1, 2)]
     low = lax.broadcasted_iota(jnp.int32, (half, 2 * HDA), 1) < HDA
     scores = cross_scores(0)
     for i in range(n):
@@ -565,14 +575,8 @@
             to_mate(1, i)
 
     r_rest[pl.ds(mine, 1)] = o_rest[pl.ds(h, 1)]
-    with scope("T4weights"):
-        @pl.when(inner)
-        def _():
-            for i in range(3):
-                pass_weights(i)
-
     ends, peers = [lax.rem(w, 2)], [lax.rem(w + 1, 2)]
-    with scope("T4forward"):
+    with scope("T4outer"):
         for i in range(n):
             to_plane(2, i)
 
@@ -582,23 +586,13 @@
                 for i in range(n):
                     to_mate(kind, i)
             exchange_rest(across_side)
+            for i in range(3):
+                pass_weights(i)
 
         @pl.when(inner)
         def _():
             for i in range(n):
-                forward(1, i, ends)
-            for i in range(n):
                 to_across(2, i)
-                to_mate(2, i)
-            for kind, ks in ((1, peers), (2, ends), (2, peers)):
-                for i in range(n):
-                    forward(kind, i, ks)
-
-    with scope("T5pass"):
-        @pl.when(outer)
-        def _():
-            for i in range(3):
-                pass_weights(i)
 
     with scope("T5w"):
         own[3].wait()
@@ -606,6 +600,12 @@
         settle_weights(0)
     with scope("T6self"):
         gathered(0)
+
+    @pl.when(outer)
+    def _():
+        for i in range(n):
+            to_across(1, i)
+
     heads = n * n
     joined = jnp.concatenate([r_self[s] for s in range(heads)], 1)
     totals[...] = jnp.dot(
@@ -614,9 +614,21 @@
 
     @pl.when(outer)
     def _():
-        for kind in (1, 2):
+        with scope("T7m"):
+            settle(many(1, n), m_recv.at[1])
+        for i in range(n):
+            to_across(2, i)
+
+    with scope("T7forward"):
+        @pl.when(inner)
+        def _():
             for i in range(n):
-                to_across(kind, i)
+                forward(1, i, ends)
+            for i in range(n):
+                to_mate(2, i)
+            pass_weights(2)
+            for i in range(n):
+                forward(1, i, peers)
 
     with scope("T7w"):
         settle_weights(1)
@@ -670,6 +682,13 @@
         for b in (n // 2 - 1 - u, n // 2 + u):
             deliver(0, b)
         if u == 0:
+            with scope("T8forward"):
+                @pl.when(inner)
+                def _():
+                    for ks in (ends, peers):
+                        for i in range(n):
+                            forward(2, i, ks)
+
             with scope("T8weights"):
                 settle_weights(2)
             audio_joined = jnp.concatenate([r_rest[s, : n * part_few, :] for s in range(heads)], 1)

time: 78.2 us -> 76.4 us (0.977)
  the two profiles are of different devices: /device:TPU:2 before, /device:TPU:1 now
where the time goes in v4:
time: 76.4 us; the launch traced here: 76.2 us
  Pallas kernels  73.9 us (97%)
  other arithmetic  1.64 us (2%)
    pallas_call x1, Pallas kernels, shards(): pl.pallas_call(functools.partial(joint_kernel, n), out_shape=(jax.ShapeDt...  73.9 us
    convert_element_type x2, other arithmetic, shards(): return (video_out.astype(bf16), audio_out.astype(bf16))  1.64 us

profile of v4, /device:TPU:1, one launch (start us, length us, event | category | flops | bytes accessed | tf_op | source)
XLA Modules:
  0.0 76.2 jit_solution(4715590573409680344)
XLA Ops:
  0.6 0.0 copy-start
  0.6 73.9 %joint.1 = (bf16[256,1024]{1,0:T(8,128)(2,1)S(1)}, bf16[64,512]{1,0:T(8,128)(2,1)S(1)}) custom-call(bf16[256,512]{1,0:T(8,128)(2,1)} %vq.1, bf16[256,512]{1,0:T(8,128)(2,1)} %vk.1, bf16[256,512]{1,0:T(8,128)(2,1)} %vv.1, bf16[256,256]{1,0:T(8,128)(2,1)} %cvq.1, bf16[256,256]{1,0:T(8,128)(2,1)} %cvk.1, bf16[256,256]{1,0:T(8,128)(2,1)} %cvv.1, ...), custom_call_target="tpu_custom_call" | custom-call | tf_op jit(solution)/shard_map/joint/pallas_call | solution.py:740
  74.5 0.0 copy-done
  74.5 0.0 copy-start.1
  74.6 1.0 %add_convert_fusion = bf16[256,1024]{1,0:T(8,128)(2,1)} fusion(bf16[256,1024]{1,0:T(8,128)(2,1)S(1)} %get-tuple-element.4, bf16[256,1024]{1,0:T(8,128)(2,1)S(1)} %copy-done), kind=kLoop, calls=%fused_computation | loop fusion | flops 1048576 | bytes 1572864 | tf_op jit(solution)/shard_map/convert_element_type | solution.py:790
  75.5 0.0 copy-done.1
  75.5 0.6 add_convert_fusion.1
Async XLA Ops:
  0.6 73.9 %copy-start = (bf16[256,1024]{1,0:T(8,128)(2,1)S(1)}, bf16[256,1024]{1,0:T(8,128)(2,1)}, u32[]{:S(2)}) copy-start(bf16[256,1024]{1,0:T(8,128)(2,1)} %param.19) | copy-start | bytes 1572868
  74.5 1.0 %copy-start.1 = (bf16[64,512]{1,0:T(8,128)(2,1)S(1)}, bf16[64,512]{1,0:T(8,128)(2,1)}, u32[]{:S(2)}) copy-start(bf16[64,512]{1,0:T(8,128)(2,1)} %param.20) | copy-start | bytes 196612

commit v5 on v3

--- a/solution.py
+++ b/solution.py
@@ -270,7 +270,7 @@
         ]
         + [
             pltpu.make_async_copy(source, few_stage.at[i], local.at[3 + i])
-            for i, source in enumerate((cak, caq, av, aq, cav, ak))
+            for i, source in enumerate((cak, cav, caq, aq, av, ak))
         ]
     )
     own = start(
@@ -347,30 +347,35 @@
 
     for copy in staged:
         copy.wait()
+    later = half + few
     for j in range(n):
         cols = slice(j * HDA, (j + 1) * HDA)
-        pack[j, :rows, :] = jnp.concatenate([wide_stage[0, :, cols], wide_stage[1, :, cols]], 1)
-        pack[j, rows : rows + half, :] = jnp.concatenate(
-            [wide_stage[2, :half, cols], wide_stage[2, half:, cols]], 1
-        )
-        for k in range(3):
-            at = rows + half + k * few
-            pack[j, at : at + few, :] = jnp.concatenate(
-                [few_stage[2 * k, :, cols], few_stage[2 * k + 1, :, cols]], 1
+        for begin, k in ((0, 0), (later, 1), (later + half, 2)):
+            pack[j, begin : begin + half, :] = jnp.concatenate(
+                [wide_stage[k, :half, cols], wide_stage[k, half:, cols]], 1
             )
-
-    def exchange_rest(target):
+        for begin, k in ((half, 0), (later + 2 * half, 2), (later + 2 * half + few, 4)):
+            pack[j, begin : begin + few, :] = jnp.concatenate(
+                [few_stage[k, :, cols], few_stage[k + 1, :, cols]], 1
+            )
+
+    portions = (slice(0, later), slice(later, depth))
+
+    def exchange_rest(target, k):
         remote(
-            pack.at[target], p_all.at[w], a_send.at[3], a_recv.at[3], {"wide": target, "heads": h}
+            pack.at[target, portions[k]], p_all.at[w, portions[k]], a_send.at[3 + k],
+            a_recv.at[3 + k], {"wide": target, "heads": h},
         ).start()
 
     outer = jnp.logical_not(inner)
-    exchange_rest(mate)
+    exchange_rest(mate, 0)
+    exchange_rest(mate, 1)
 
     @pl.when(outer)
     def _():
-        exchange_rest(far_end)
-
+        exchange_rest(far_end, 0)
+        exchange_rest(far_end, 1)
+        exchange_rest(across_side, 0)
 
     own_pack = pltpu.make_async_copy(pack.at[w], p_all.at[w], local.at[0])
     own_pack.start()
@@ -387,12 +392,14 @@
             tall_bias[i * part_rows : (i + 1) * part_rows, j * few : (j + 1) * few] = jnp.full(
                 (part_rows, few), drop
             )
-            wide_bias[j * few : (j + 1) * few, i * rows : (i + 1) * rows] = jnp.full(
-                (few, rows), drop
-            )
-
-    splits = (part_few * n + half // 2, half // 2)
-    starts = (0, splits[0])
+            for k in range(2):
+                begin = (k * n + i) * half
+                wide_bias[j * few : (j + 1) * few, begin : begin + half] = jnp.full(
+                    (few, half), drop
+                )
+
+    splits = (half // 2, half // 2, n * part_few)
+    starts = (n * part_few, n * part_few + half // 2, 0)
 
     def chunk(ref, kind):
         if kind == 0:
@@ -474,7 +481,9 @@
 
     @pl.when(inner)
     def _():
-        exchange_rest(far_end)
+        exchange_rest(far_end, 0)
+        exchange_rest(far_end, 1)
+        exchange_rest(across_side, 0)
 
     keys = k_all[...].reshape(n * rows, HDV)
     values = v_all[...].reshape(n * rows, HDV)
@@ -494,59 +503,43 @@
         to_across(0, i)
         to_mate(0, i)
     r_self[pl.ds(mine, 1)] = o_self[pl.ds(h, 1)]
-
-    @pl.when(inner)
-    def _():
-        exchange_rest(across_side)
+    ends, peers = [lax.rem(w, 2)], [lax.rem(w + 1, 2)]
 
     with scope("T2weights"):
         swap_weights(0)
         swap_weights(1)
-    with scope("T2forward"):
+    with scope("T2ends"):
         @pl.when(inner)
         def _():
-            for k in (lax.rem(w, 2), lax.rem(w + 1, 2)):
-                for i in range(n):
-                    forward(0, i, [k])
-
-    swap_weights(2)
-    with scope("T3rest"):
+            for i in range(n):
+                forward(0, i, ends)
+
+    with scope("T2video"):
         own_pack.wait()
-        settle(p_all.at[: n - 1], a_recv.at[3])
-
-    at = rows + half
+        settle(p_all.at[: n - 1, portions[0]], a_recv.at[3])
     lane = lax.broadcasted_iota(jnp.int32, (n * few, 2 * HDA), 1)
     left = lane < HDA
-    both = p_all[:, :rows, :].reshape(n * rows, 2 * HDA)
-    vals = p_all[:, rows:at, :].reshape(n * half, 2 * HDA)
-    keyed = p_all[:, at : at + few, :].reshape(n * few, 2 * HDA)
-    asked = p_all[:, at + few : at + 2 * few, :].reshape(n * few, 2 * HDA)
-    third = p_all[:, at + 2 * few : depth, :].reshape(n * few, 2 * HDA)
-    zero = jnp.zeros_like(keyed)
-    key_left = jnp.where(left, keyed, zero)
-    query_right = jnp.where(left, zero, keyed)
-    key_right = jnp.where(left, zero, third)
-    twice = jnp.concatenate([third[:, :HDA], third[:, :HDA]], 1)
-
-    scores_a = scored(asked, key_right)
-    scores_c = scored(query_right, both) + wide_bias[...]
-    weights, sums = softmax(scores_a, HDA)
-    audio_own = mixed(weights, asked) / sums
-    weights, sums = softmax(scores_c, HDA)
-    upper = jnp.concatenate([weights[:, j * rows : j * rows + half] for j in range(n)], 1)
-    lower = jnp.concatenate([weights[:, j * rows + half : (j + 1) * rows] for j in range(n)], 1)
-    audio_other = (pltpu.roll(mixed(upper, vals), HDA, 1) + mixed(lower, vals)) / sums
-    audio = jnp.where(left, audio_own, audio_other).astype(bf16)
-    for t in range(n):
-        o_rest[t, : n * part_few, :] = jnp.concatenate(
-            [audio[j * few + t * part_few : j * few + (t + 1) * part_few, :] for j in range(n)], 0
-        )
+
+    def swapped(block):
+        return jnp.concatenate([block[:, HDA:], block[:, :HDA]], 1)
+
+    def only(block, keep_left):
+        zero = jnp.zeros_like(block)
+        return jnp.where(left, block, zero) if keep_left else jnp.where(left, zero, block)
+
+    keyed = p_all[:, half:later, :].reshape(n * few, 2 * HDA)
+    key_left, key_right = only(keyed, True), only(swapped(keyed), False)
+    twice = jnp.concatenate([keyed[:, HDA:], keyed[:, HDA:]], 1)
+
     def cross_scores(i):
-        begin = pl.multiple_of(moved(turn_of(i)) * part_rows, part_rows)
+        part = moved(turn_of(i))
+        begin = pl.multiple_of(lax.rem(part, n // 2) * part_rows, part_rows)
         queries = p_all[:, pl.ds(begin, part_rows), :].reshape(rows, 2 * HDA)
-        return scored(queries, key_left) + tall_bias[...]
+        chosen = jnp.where(part < n // 2, key_left, key_right)
+        return scored(queries, chosen) + tall_bias[...]
 
     low = lax.broadcasted_iota(jnp.int32, (half, 2 * HDA), 1) < HDA
+    tail = n * part_few
     scores = cross_scores(0)
     for i in range(n):
         following = cross_scores(i + 1) if i + 1 < n else None
@@ -556,45 +549,74 @@
         block = moved(turn_of(i))
         upper = [result[j * part_rows : (j + 1) * part_rows] for j in reversed(range(n // 2))]
         packed = jnp.where(low, jnp.concatenate(upper, 0), result[half:]).astype(bf16)
-        o_rest[pl.ds(block, 1), n * part_few :, :] = packed[None]
-        to_plane(1, i)
+        o_rest[pl.ds(block, 1), tail:, :] = packed[None]
+        for kind in (1, 2):
+            to_plane(kind, i)
 
         @pl.when(inner)
         def _():
-            to_across(1, i)
-            to_mate(1, i)
-
-    r_rest[pl.ds(mine, 1)] = o_rest[pl.ds(h, 1)]
-    with scope("T4weights"):
+            for kind in (1, 2):
+                to_across(kind, i)
+                to_mate(kind, i)
+
+    r_rest[pl.ds(mine, 1), tail:, :] = o_rest[pl.ds(h, 1), tail:, :]
+
+    @pl.when(outer)
+    def _():
+        for kind in (1, 2):
+            for i in range(n):
+                to_mate(kind, i)
+
+    exchange_rest(across_side, 1)
+    with scope("T2peers"):
         @pl.when(inner)
         def _():
-            for i in range(3):
+            for i in range(n):
+                forward(0, i, peers)
+            for i in range(2):
                 pass_weights(i)
 
-    ends, peers = [lax.rem(w, 2)], [lax.rem(w + 1, 2)]
-    with scope("T4forward"):
-        for i in range(n):
-            to_plane(2, i)
-
-        @pl.when(outer)
+    swap_weights(2)
+    with scope("T3peers"):
+        @pl.when(inner)
         def _():
             for kind in (1, 2):
                 for i in range(n):
-                    to_mate(kind, i)
-            exchange_rest(across_side)
-
-        @pl.when(inner)
-        def _():
-            for i in range(n):
-                forward(1, i, ends)
-            for i in range(n):
-                to_across(2, i)
-                to_mate(2, i)
-            for kind, ks in ((1, peers), (2, ends), (2, peers)):
-                for i in range(n):
-                    forward(kind, i, ks)
-
-    with scope("T5pass"):
+                    forward(kind, i, peers)
+
+    with scope("T3rest"):
+        settle(p_all.at[: n - 1, portions[1]], a_recv.at[4])
+    begin = later
+    both = p_all[:, begin : begin + half, :].reshape(n * half, 2 * HDA)
+    vals = p_all[:, begin + half : begin + 2 * half, :].reshape(n * half, 2 * HDA)
+    begin += 2 * half
+    asked = p_all[:, begin : begin + few, :].reshape(n * few, 2 * HDA)
+    third = p_all[:, begin + few : depth, :].reshape(n * few, 2 * HDA)
+    scores_a = scored(asked, only(third, False))
+    scores_c = jnp.concatenate(
+        [scored(only(asked, True), both), scored(only(swapped(asked), False), both)], 1
+    ) + wide_bias[...]
+    weights, sums = softmax(scores_a, HDA)
+    audio_own = mixed(weights, third) / sums
+    weights, sums = softmax(scores_c, HDA)
+    upper, lower = weights[:, : n * half], weights[:, n * half :]
+    audio_other = (pltpu.roll(mixed(upper, vals), HDA, 1) + mixed(lower, vals)) / sums
+    audio = jnp.where(left, audio_own, audio_other).astype(bf16)
+    for t in range(n):
+        o_rest[t, :tail, :] = jnp.concatenate(
+            [audio[j * few + t * part_few : j * few + (t + 1) * part_few, :] for j in range(n)], 0
+        )
+    r_rest[pl.ds(mine, 1), :tail, :] = o_rest[pl.ds(h, 1), :tail, :]
+    for i in range(n):
+        to_plane(3, i)
+        to_mate(3, i)
+
+    @pl.when(inner)
+    def _():
+        for i in range(n):
+            to_across(3, i)
+
+    with scope("T4pass"):
         @pl.when(outer)
         def _():
             for i in range(3):
@@ -606,17 +628,26 @@
         settle_weights(0)
     with scope("T6self"):
         gathered(0)
+
+    @pl.when(outer)
+    def _():
+        for kind in (1, 2, 3):
+            for i in range(n):
+                to_across(kind, i)
+
     heads = n * n
     joined = jnp.concatenate([r_self[s] for s in range(heads)], 1)
     totals[...] = jnp.dot(
         joined, ws_all[...].reshape(-1, ws.shape[1]), preferred_element_type=jnp.float32
     )
 
-    @pl.when(outer)
-    def _():
-        for kind in (1, 2):
-            for i in range(n):
-                to_across(kind, i)
+    with scope("T7forward"):
+        @pl.when(inner)
+        def _():
+            for kind in (1, 2):
+                for i in range(n):
+                    forward(kind, i, ends)
+            pass_weights(2)
 
     with scope("T7w"):
         settle_weights(1)
@@ -643,7 +674,7 @@
     for u in range(2):
         with scope("T8gather%d" % u):
             gathered(1 + u)
-        begin = n * part_few + u * (half // 2)
+        begin = tail + u * (half // 2)
         piece = slice(begin, begin + half // 2)
         crossed = jnp.concatenate(
             [
@@ -660,41 +691,48 @@
             sum_v[where, :] = (
                 totals[where, :] + products[k * size : (k + 1) * size, :]
             ).astype(bf16)
-        if u == 1:
-            with scope("T8sent"):
-                @pl.when(inner)
-                def _():
-                    for kind in range(3):
-                        settle(many(kind, 2 * n), r_send.at[kind])
-
         for b in (n // 2 - 1 - u, n // 2 + u):
             deliver(0, b)
         if u == 0:
-            with scope("T8weights"):
-                settle_weights(2)
-            audio_joined = jnp.concatenate([r_rest[s, : n * part_few, :] for s in range(heads)], 1)
-            sum_a[...] = jnp.dot(
-                audio_joined, wa_all[...].reshape(-1, aso.shape[1]),
-                preferred_element_type=jnp.float32,
-            ).astype(bf16)
-            for b in range(n):
-                deliver(1, b)
+            with scope("T7audio"):
+                @pl.when(inner)
+                def _():
+                    for ks in (ends, peers):
+                        for i in range(n):
+                            forward(3, i, ks)
+
+    with scope("T8audio"):
+        settle_weights(2)
+        gathered(3)
+    audio_joined = jnp.concatenate([r_rest[s, :tail, :] for s in range(heads)], 1)
+    sum_a[...] = jnp.dot(
+        audio_joined, wa_all[...].reshape(-1, aso.shape[1]), preferred_element_type=jnp.float32
+    ).astype(bf16)
+    for b in range(n):
+        deliver(1, b)
 
     with scope("T9results"):
         settle(out_v, e_recv.at[0])
         settle(out_a, e_recv.at[1])
 
     with scope("TBsends"):
-        for i, target in enumerate((q_all, k_all, v_all, p_all)):
+        for i, target in enumerate((q_all, k_all, v_all)):
             settle(target.at[: n - 1], a_send.at[i])
+        for k, portion in enumerate(portions):
+            settle(p_all.at[: n - 1, portion], a_send.at[3 + k])
         for i in range(3):
             settle(part_of(targets[i].at[h], g), w_send.at[i, 0])
             settle(targets[i].at[h], w_send.at[i, 1])
             settle(part_of(targets[i].at[h], g), w_send.at[i, 2])
             settle(targets[i].at[h], w_send.at[i, 3])
-        for kind in range(3):
+        for kind in range(4):
             settle(many(kind, n - 1), x_send.at[kind])
             settle(many(kind, 2 * n), z_send.at[kind])
+        @pl.when(inner)
+        def _():
+            for kind in range(4):
+                settle(many(kind, 2 * n), r_send.at[kind])
+
         for c, (ref, size) in enumerate(((sum_v, part_rows), (sum_a, part_few))):
             settle(ref.at[: (n - 1) * size], e_send.at[c])
 
@@ -747,10 +785,10 @@
             pltpu.VMEM(video_hidden.shape, f32),
             pltpu.VMEM(video_hidden.shape, bf16),
             pltpu.VMEM(audio_hidden.shape, bf16),
+            dma((5,)), dma((5,)),
+            dma((3, 4)), dma((3, 4)),
             dma((4,)), dma((4,)),
-            dma((3, 4)), dma((3, 4)),
-            dma((3,)), dma((3,)),
-            dma((3,)), dma((3, n, 2)), dma((3,)), dma((3,)),
+            dma((4,)), dma((4, n, 2)), dma((4,)), dma((4,)),
             dma((2,)), dma((2,)),
             dma((18,)),
         ],

time: 78.2 us -> 75 us (0.959)
  the two profiles are of different devices: /device:TPU:2 before, /device:TPU:1 now
where the time goes in v5:
time: 75 us; the launch traced here: 74.9 us
  Pallas kernels  72.6 us (97%)
  other arithmetic  1.64 us (2%)
    pallas_call x1, Pallas kernels, shards(): pl.pallas_call(functools.partial(joint_kernel, n), out_shape=(jax.ShapeDt...  72.6 us
    convert_element_type x2, other arithmetic, shards(): return (video_out.astype(bf16), audio_out.astype(bf16))  1.64 us

profile of v5, /device:TPU:1, one launch (start us, length us, event | category | flops | bytes accessed | tf_op | source)
XLA Modules:
  0.0 74.9 jit_solution(3414385317381368496)
XLA Ops:
  0.6 0.0 copy-start
  0.6 72.6 %joint.1 = (bf16[256,1024]{1,0:T(8,128)(2,1)S(1)}, bf16[64,512]{1,0:T(8,128)(2,1)S(1)}) custom-call(bf16[256,512]{1,0:T(8,128)(2,1)} %vq.1, bf16[256,512]{1,0:T(8,128)(2,1)} %vk.1, bf16[256,512]{1,0:T(8,128)(2,1)} %vv.1, bf16[256,256]{1,0:T(8,128)(2,1)} %cvq.1, bf16[256,256]{1,0:T(8,128)(2,1)} %cvk.1, bf16[256,256]{1,0:T(8,128)(2,1)} %cvv.1, ...), custom_call_target="tpu_custom_call" | custom-call | tf_op jit(solution)/shard_map/joint/pallas_call | solution.py:759
  73.2 0.0 copy-done
  73.2 0.0 copy-start.1
  73.2 1.0 %add_convert_fusion = bf16[256,1024]{1,0:T(8,128)(2,1)} fusion(bf16[256,1024]{1,0:T(8,128)(2,1)S(1)} %get-tuple-element.4, bf16[256,1024]{1,0:T(8,128)(2,1)S(1)} %copy-done), kind=kLoop, calls=%fused_computation | loop fusion | flops 1048576 | bytes 1572864 | tf_op jit(solution)/shard_map/convert_element_type | solution.py:809
  74.2 0.0 copy-done.1
  74.2 0.6 add_convert_fusion.1
Async XLA Ops:
  0.6 72.6 %copy-start = (bf16[256,1024]{1,0:T(8,128)(2,1)S(1)}, bf16[256,1024]{1,0:T(8,128)(2,1)}, u32[]{:S(2)}) copy-start(bf16[256,1024]{1,0:T(8,128)(2,1)} %param.19) | copy-start | bytes 1572868
  73.2 1.0 %copy-start.1 = (bf16[64,512]{1,0:T(8,128)(2,1)S(1)}, bf16[64,512]{1,0:T(8,128)(2,1)}, u32[]{:S(2)}) copy-start(bf16[64,512]{1,0:T(8,128)(2,1)} %param.20) | copy-start | bytes 196612

commit v6 on v5

--- a/solution.py
+++ b/solution.py
@@ -210,7 +210,7 @@
     out_v, out_a,
     q_all, k_all, v_all, self_stage, wide_stage, few_stage, pack, p_all, ws_all, wc_all, wa_all,
     tall_bias, wide_bias, o_self, o_rest, r_self, r_rest, totals, sum_v, sum_a,
-    a_send, a_recv, w_send, w_recv, x_send, x_recv, z_send, z_recv, m_recv, r_send,
+    a_send, a_recv, w_send, w_recv, x_recv, z_send, z_recv, m_recv, r_send,
     e_send, e_recv, local,
 ):
     g = lax.axis_index("groups")
@@ -259,27 +259,27 @@
     streams = ((vq, q_all), (vk, k_all), (vv, v_all))
     self_staged = start(
         [
-            pltpu.make_async_copy(source, self_stage.at[i], local.at[15 + i])
+            pltpu.make_async_copy(source, self_stage.at[i], local.at[2])
             for i, (source, _) in enumerate(streams)
         ]
     )
     staged = start(
         [
-            pltpu.make_async_copy(source, wide_stage.at[i], local.at[i])
+            pltpu.make_async_copy(source, wide_stage.at[i], local.at[0])
             for i, source in enumerate((cvq, cvk, cvv))
         ]
         + [
-            pltpu.make_async_copy(source, few_stage.at[i], local.at[3 + i])
+            pltpu.make_async_copy(source, few_stage.at[i], local.at[1])
             for i, source in enumerate((cak, cav, caq, aq, av, ak))
         ]
     )
     own = start(
         [
-            pltpu.make_async_copy(head_cols(source, w), target.at[w], local.at[9 + i])
+            pltpu.make_async_copy(head_cols(source, w), target.at[w], local.at[3])
             for i, (source, target) in enumerate(streams)
         ]
         + [
-            pltpu.make_async_copy(source, target.at[h], local.at[12 + i])
+            pltpu.make_async_copy(source, target.at[h], local.at[4 + i])
             for i, (source, target) in enumerate(((ws, ws_all), (wc, wc_all)))
         ]
     )
@@ -287,11 +287,10 @@
         for k, source in enumerate((aso, aco)):
             at = (2 * j + k) * HDA
             pltpu.make_async_copy(
-                source.at[j * HDA : (j + 1) * HDA], wa_all.at[h, at : at + HDA], local.at[14]
+                source.at[j * HDA : (j + 1) * HDA], wa_all.at[h, at : at + HDA], local.at[6]
             ).start()
-    own.append(pltpu.make_async_copy(wa_all.at[h], wa_all.at[h], local.at[14]))
-    for copy in self_staged:
-        copy.wait()
+    own.append(pltpu.make_async_copy(wa_all.at[h], wa_all.at[h], local.at[6]))
+    settle(self_stage, local.at[2])
     with scope("T0barrier"):
         pl.semaphore_wait(barrier, len(others) + 1)
 
@@ -321,21 +320,21 @@
     def send_weights(i):
         remote(
             part_of(sources[i], g), part_of(targets[i].at[h], g),
-            w_send.at[i, 0], w_recv.at[i, 0], {"wide": w, "heads": opposite},
+            w_send.at[i], w_recv.at[i, 0], {"wide": w, "heads": opposite},
         ).start()
 
     def share_weights(i):
-        remote(sources[i], targets[i].at[h], w_send.at[i, 1], w_recv.at[i, 1], partner).start()
+        remote(sources[i], targets[i].at[h], w_send.at[i], w_recv.at[i, 1], partner).start()
 
     def swap_weights(i):
         piece = part_of(targets[i].at[opposite], g)
         settle(piece, w_recv.at[i, 0])
-        remote(piece, piece, w_send.at[i, 2], w_recv.at[i, 2], twin).start()
+        remote(piece, piece, w_send.at[i], w_recv.at[i, 2], twin).start()
 
     def pass_weights(i):
         slot = targets[i].at[opposite]
         settle(part_of(slot, 1 - g), w_recv.at[i, 2])
-        remote(slot, slot, w_send.at[i, 3], w_recv.at[i, 3], partner).start()
+        remote(slot, slot, w_send.at[i], w_recv.at[i, 3], partner).start()
 
     def settle_weights(i):
         settle(targets[i].at[h], w_recv.at[i, 1])
@@ -345,8 +344,8 @@
         send_weights(i)
         share_weights(i)
 
-    for copy in staged:
-        copy.wait()
+    settle(wide_stage, local.at[0])
+    settle(few_stage, local.at[1])
     later = half + few
     for j in range(n):
         cols = slice(j * HDA, (j + 1) * HDA)
@@ -377,7 +376,7 @@
         exchange_rest(far_end, 1)
         exchange_rest(across_side, 0)
 
-    own_pack = pltpu.make_async_copy(pack.at[w], p_all.at[w], local.at[0])
+    own_pack = pltpu.make_async_copy(pack.at[w], p_all.at[w], local.at[7])
     own_pack.start()
     own.pop().wait()
     send_weights(2)
@@ -429,7 +428,7 @@
         @pl.when(part != h)
         def _():
             remote(
-                piece, where, x_send.at[kind], x_recv.at[kind], {"wide": w, "heads": part}
+                piece, where, z_send.at[kind], x_recv.at[kind], {"wide": w, "heads": part}
             ).start()
 
     def to_across(kind, i):
@@ -475,8 +474,8 @@
                     settle(far_piece(kind, d, k), z_recv.at[kind, d, k])
 
     with scope("T1self"):
+        settle(q_all.at[: len(streams)], local.at[3])
         for i, target in enumerate((q_all, k_all, v_all)):
-            own[i].wait()
             settle(target.at[: n - 1], a_recv.at[i])
 
     @pl.when(inner)
@@ -691,15 +690,24 @@
             sum_v[where, :] = (
                 totals[where, :] + products[k * size : (k + 1) * size, :]
             ).astype(bf16)
-        for b in (n // 2 - 1 - u, n // 2 + u):
-            deliver(0, b)
         if u == 0:
-            with scope("T7audio"):
-                @pl.when(inner)
-                def _():
-                    for ks in (ends, peers):
-                        for i in range(n):
-                            forward(3, i, ks)
+            for b in (n // 2 - 1, n // 2):
+                deliver(0, b)
+    with scope("T7audio"):
+        @pl.when(inner)
+        def _():
+            for ks in (ends, peers):
+                for i in range(n):
+                    forward(3, i, ks)
+
+    @pl.when(inner)
+    def _():
+        deliver(0, mate)
+        deliver(0, far_end)
+
+    @pl.when(outer)
+    def _():
+        deliver(0, w)
 
     with scope("T8audio"):
         settle_weights(2)
@@ -711,6 +719,11 @@
     for b in range(n):
         deliver(1, b)
 
+    @pl.when(outer)
+    def _():
+        deliver(0, far_end)
+
+
     with scope("T9results"):
         settle(out_v, e_recv.at[0])
         settle(out_a, e_recv.at[1])
@@ -721,13 +734,9 @@
         for k, portion in enumerate(portions):
             settle(p_all.at[: n - 1, portion], a_send.at[3 + k])
         for i in range(3):
-            settle(part_of(targets[i].at[h], g), w_send.at[i, 0])
-            settle(targets[i].at[h], w_send.at[i, 1])
-            settle(part_of(targets[i].at[h], g), w_send.at[i, 2])
-            settle(targets[i].at[h], w_send.at[i, 3])
+            settle(targets[i].at[:3], w_send.at[i])
         for kind in range(4):
-            settle(many(kind, n - 1), x_send.at[kind])
-            settle(many(kind, 2 * n), z_send.at[kind])
+            settle(many(kind, 3 * n - 1), z_send.at[kind])
         @pl.when(inner)
         def _():
             for kind in range(4):
@@ -786,11 +795,11 @@
             pltpu.VMEM(video_hidden.shape, bf16),
             pltpu.VMEM(audio_hidden.shape, bf16),
             dma((5,)), dma((5,)),
-            dma((3, 4)), dma((3, 4)),
-            dma((4,)), dma((4,)),
+            dma((3,)), dma((3, 4)),
+            dma((4,)),
             dma((4,)), dma((4, n, 2)), dma((4,)), dma((4,)),
             dma((2,)), dma((2,)),
-            dma((18,)),
+            dma((8,)),
         ],
         compiler_params=pltpu.CompilerParams(
             collective_id=0, has_side_effects=True, vmem_limit_bytes=48 * 1024 * 1024

time: 75 us -> 74.9 us (level)
  no operation moved by 1% of the time
where the time goes in v6:
time: 74.9 us; the launch traced here: 74.7 us
  Pallas kernels  72.4 us (97%)
  other arithmetic  1.64 us (2%)
    pallas_call x1, Pallas kernels, shards(): pl.pallas_call(functools.partial(joint_kernel, n), out_shape=(jax.ShapeDt...  72.4 us
    convert_element_type x2, other arithmetic, shards(): return (video_out.astype(bf16), audio_out.astype(bf16))  1.64 us

profile of v6, /device:TPU:1, one launch (start us, length us, event | category | flops | bytes accessed | tf_op | source)
XLA Modules:
  0.0 74.7 jit_solution(282603943679025946)
XLA Ops:
  0.6 0.0 copy-start
  0.6 72.4 %joint.1 = (bf16[256,1024]{1,0:T(8,128)(2,1)S(1)}, bf16[64,512]{1,0:T(8,128)(2,1)S(1)}) custom-call(bf16[256,512]{1,0:T(8,128)(2,1)} %vq.1, bf16[256,512]{1,0:T(8,128)(2,1)} %vk.1, bf16[256,512]{1,0:T(8,128)(2,1)} %vv.1, bf16[256,256]{1,0:T(8,128)(2,1)} %cvq.1, bf16[256,256]{1,0:T(8,128)(2,1)} %cvk.1, bf16[256,256]{1,0:T(8,128)(2,1)} %cvv.1, ...), custom_call_target="tpu_custom_call" | custom-call | tf_op jit(solution)/shard_map/joint/pallas_call | solution.py:768
  73.1 0.0 copy-done
  73.1 0.0 copy-start.1
  73.1 1.0 %add_convert_fusion = bf16[256,1024]{1,0:T(8,128)(2,1)} fusion(bf16[256,1024]{1,0:T(8,128)(2,1)S(1)} %get-tuple-element.4, bf16[256,1024]{1,0:T(8,128)(2,1)S(1)} %copy-done), kind=kLoop, calls=%fused_computation | loop fusion | flops 1048576 | bytes 1572864 | tf_op jit(solution)/shard_map/convert_element_type | solution.py:818
  74.1 0.0 copy-done.1
  74.1 0.6 add_convert_fusion.1
Async XLA Ops:
  0.6 72.4 %copy-start = (bf16[256,1024]{1,0:T(8,128)(2,1)S(1)}, bf16[256,1024]{1,0:T(8,128)(2,1)}, u32[]{:S(2)}) copy-start(bf16[256,1024]{1,0:T(8,128)(2,1)} %param.19) | copy-start | bytes 1572868
  73.1 1.0 %copy-start.1 = (bf16[64,512]{1,0:T(8,128)(2,1)S(1)}, bf16[64,512]{1,0:T(8,128)(2,1)}, u32[]{:S(2)}) copy-start(bf16[64,512]{1,0:T(8,128)(2,1)} %param.20) | copy-start | bytes 196612

commit v7 on v6

--- a/solution.py
+++ b/solution.py
@@ -206,12 +206,12 @@
 
 def joint_kernel(
     n,
-    vq, vk, vv, cvq, cvk, cvv, aq, ak, av, caq, cak, cav, ws, wc, aso, aco, table,
+    vq, vk, vv, cvq, cvk, cvv, aq, ak, av, caq, cak, cav, ws, wc, aso, aco, table_in,
     out_v, out_a,
     q_all, k_all, v_all, self_stage, wide_stage, few_stage, pack, p_all, ws_all, wc_all, wa_all,
     tall_bias, wide_bias, o_self, o_rest, r_self, r_rest, totals, sum_v, sum_a,
     a_send, a_recv, w_send, w_recv, x_recv, z_send, z_recv, m_recv, r_send,
-    e_send, e_recv, local,
+    e_send, e_recv, table, local,
 ):
     g = lax.axis_index("groups")
     w = lax.axis_index("wide")
@@ -257,6 +257,8 @@
         return copies
 
     streams = ((vq, q_all), (vk, k_all), (vv, v_all))
+    table_copy = pltpu.make_async_copy(table_in, table, local.at[8])
+    table_copy.start()
     self_staged = start(
         [
             pltpu.make_async_copy(source, self_stage.at[i], local.at[2])
@@ -382,6 +384,7 @@
     send_weights(2)
     share_weights(2)
 
+    table_copy.wait()
     for i in range(n):
         for j in range(n):
             column = j - i + REACH
@@ -771,7 +774,7 @@
             jax.ShapeDtypeStruct(video_hidden.shape, bf16),
             jax.ShapeDtypeStruct(audio_hidden.shape, bf16),
         ),
-        in_specs=[pl.BlockSpec(memory_space=pltpu.HBM)] * 16 + [pl.BlockSpec(memory_space=pltpu.SMEM)],
+        in_specs=[pl.BlockSpec(memory_space=pltpu.HBM)] * 17,
         out_specs=(anywhere, anywhere),
         scratch_shapes=[
             pltpu.VMEM((n, rows, HDV), bf16),
@@ -799,7 +802,8 @@
             dma((4,)),
             dma((4,)), dma((4, n, 2)), dma((4,)), dma((4,)),
             dma((2,)), dma((2,)),
-            dma((8,)),
+            pltpu.SMEM(table.shape, jnp.int32),
+            dma((9,)),
         ],
         compiler_params=pltpu.CompilerParams(
             collective_id=0, has_side_effects=True, vmem_limit_bytes=48 * 1024 * 1024

time: 74.9 us -> 74.1 us (0.989)
  Pallas kernels: 72.4 us -> 71.6 us
    pallas_call x1, Pallas kernels: 72.4 us -> 71.6 us  [shards(): pl.pallas_call(functools.partial(joint_kernel, n), out_shape=(jax.ShapeDt...]
where the time goes in v7:
time: 74.1 us; the launch traced here: 73.9 us
  Pallas kernels  71.6 us (97%)
  other arithmetic  1.64 us (2%)
    pallas_call x1, Pallas kernels, shards(): pl.pallas_call(functools.partial(joint_kernel, n), out_shape=(jax.ShapeDt...  71.6 us
    convert_element_type x2, other arithmetic, shards(): return (video_out.astype(bf16), audio_out.astype(bf16))  1.64 us

profile of v7, /device:TPU:1, one launch (start us, length us, event | category | flops | bytes accessed | tf_op | source)
XLA Modules:
  0.0 73.9 jit_solution(15838795361946967542)
XLA Ops:
  0.6 0.0 copy-start
  0.6 71.6 %joint.1 = (bf16[256,1024]{1,0:T(8,128)(2,1)S(1)}, bf16[64,512]{1,0:T(8,128)(2,1)S(1)}) custom-call(bf16[256,512]{1,0:T(8,128)(2,1)} %vq.1, bf16[256,512]{1,0:T(8,128)(2,1)} %vk.1, bf16[256,512]{1,0:T(8,128)(2,1)} %vv.1, bf16[256,256]{1,0:T(8,128)(2,1)} %cvq.1, bf16[256,256]{1,0:T(8,128)(2,1)} %cvk.1, bf16[256,256]{1,0:T(8,128)(2,1)} %cvv.1, ...), custom_call_target="tpu_custom_call" | custom-call | tf_op jit(solution)/shard_map/joint/pallas_call | solution.py:771
  72.3 0.0 copy-done
  72.3 0.0 copy-start.1
  72.3 1.0 %add_convert_fusion = bf16[256,1024]{1,0:T(8,128)(2,1)} fusion(bf16[256,1024]{1,0:T(8,128)(2,1)S(1)} %get-tuple-element.4, bf16[256,1024]{1,0:T(8,128)(2,1)S(1)} %copy-done), kind=kLoop, calls=%fused_computation | loop fusion | flops 1048576 | bytes 1572864 | tf_op jit(solution)/shard_map/convert_element_type | solution.py:822
  73.3 0.0 copy-done.1
  73.3 0.6 add_convert_fusion.1
Async XLA Ops:
  0.6 71.6 %copy-start = (bf16[256,1024]{1,0:T(8,128)(2,1)S(1)}, bf16[256,1024]{1,0:T(8,128)(2,1)}, u32[]{:S(2)}) copy-start(bf16[256,1024]{1,0:T(8,128)(2,1)} %param.19) | copy-start | bytes 1572868
  72.3 1.0 %copy-start.1 = (bf16[64,512]{1,0:T(8,128)(2,1)S(1)}, bf16[64,512]{1,0:T(8,128)(2,1)}, u32[]{:S(2)}) copy-start(bf16[64,512]{1,0:T(8,128)(2,1)} %param.20) | copy-start | bytes 196612

commit v8 on v7

--- a/solution.py
+++ b/solution.py
@@ -265,6 +265,24 @@
             for i, (source, _) in enumerate(streams)
         ]
     )
+    settle(self_stage, local.at[2])
+    with scope("T0barrier"):
+        pl.semaphore_wait(barrier, len(others) + 1)
+
+    far_end = (1 - side) * (n - 1)
+
+    def exchange(target):
+        for i, (_, landing) in enumerate(streams):
+            remote(
+                head_cols(self_stage.at[i], target), landing.at[w], a_send.at[i], a_recv.at[i],
+                {"wide": target, "heads": h},
+            ).start()
+
+    near = jnp.where(inner, across_side, mate)
+    last = jnp.where(inner, mate, across_side)
+    for target in (far_end, near, last):
+        exchange(target)
+
     staged = start(
         [
             pltpu.make_async_copy(source, wide_stage.at[i], local.at[0])
@@ -292,23 +310,6 @@
                 source.at[j * HDA : (j + 1) * HDA], wa_all.at[h, at : at + HDA], local.at[6]
             ).start()
     own.append(pltpu.make_async_copy(wa_all.at[h], wa_all.at[h], local.at[6]))
-    settle(self_stage, local.at[2])
-    with scope("T0barrier"):
-        pl.semaphore_wait(barrier, len(others) + 1)
-
-    far_end = (1 - side) * (n - 1)
-
-    def exchange(target):
-        for i, (_, landing) in enumerate(streams):
-            remote(
-                head_cols(self_stage.at[i], target), landing.at[w], a_send.at[i], a_recv.at[i],
-                {"wide": target, "heads": h},
-            ).start()
-
-    near = jnp.where(inner, across_side, mate)
-    last = jnp.where(inner, mate, across_side)
-    for target in (far_end, near, last):
-        exchange(target)
 
     targets = (ws_all, wc_all, wa_all)
     sources = (ws, wc, wa_all.at[h])

time: 74.1 us -> 74.1 us (level)
  no operation moved by 1% of the time
where the time goes in v8:
time: 74.1 us; the launch traced here: 73.9 us
  Pallas kernels  71.6 us (97%)
  other arithmetic  1.64 us (2%)
    pallas_call x1, Pallas kernels, shards(): pl.pallas_call(functools.partial(joint_kernel, n), out_shape=(jax.ShapeDt...  71.6 us
    convert_element_type x2, other arithmetic, shards(): return (video_out.astype(bf16), audio_out.astype(bf16))  1.64 us

profile of v8, /device:TPU:1, one launch (start us, length us, event | category | flops | bytes accessed | tf_op | source)
XLA Modules:
  0.0 73.9 jit_solution(10962884559496034180)
XLA Ops:
  0.6 0.0 copy-start
  0.6 71.6 %joint.1 = (bf16[256,1024]{1,0:T(8,128)(2,1)S(1)}, bf16[64,512]{1,0:T(8,128)(2,1)S(1)}) custom-call(bf16[256,512]{1,0:T(8,128)(2,1)} %vq.1, bf16[256,512]{1,0:T(8,128)(2,1)} %vk.1, bf16[256,512]{1,0:T(8,128)(2,1)} %vv.1, bf16[256,256]{1,0:T(8,128)(2,1)} %cvq.1, bf16[256,256]{1,0:T(8,128)(2,1)} %cvk.1, bf16[256,256]{1,0:T(8,128)(2,1)} %cvv.1, ...), custom_call_target="tpu_custom_call" | custom-call | tf_op jit(solution)/shard_map/joint/pallas_call | solution.py:772
  72.3 0.0 copy-done
  72.3 0.0 copy-start.1
  72.3 1.0 %add_convert_fusion = bf16[256,1024]{1,0:T(8,128)(2,1)} fusion(bf16[256,1024]{1,0:T(8,128)(2,1)S(1)} %get-tuple-element.4, bf16[256,1024]{1,0:T(8,128)(2,1)S(1)} %copy-done), kind=kLoop, calls=%fused_computation | loop fusion | flops 1048576 | bytes 1572864 | tf_op jit(solution)/shard_map/convert_element_type | solution.py:823
  73.3 0.0 copy-done.1
  73.3 0.6 add_convert_fusion.1
Async XLA Ops:
  0.6 71.6 %copy-start = (bf16[256,1024]{1,0:T(8,128)(2,1)S(1)}, bf16[256,1024]{1,0:T(8,128)(2,1)}, u32[]{:S(2)}) copy-start(bf16[256,1024]{1,0:T(8,128)(2,1)} %param.19) | copy-start | bytes 1572868
  72.3 1.0 %copy-start.1 = (bf16[64,512]{1,0:T(8,128)(2,1)S(1)}, bf16[64,512]{1,0:T(8,128)(2,1)}, u32[]{:S(2)}) copy-start(bf16[64,512]{1,0:T(8,128)(2,1)} %param.20) | copy-start | bytes 196612
